TPU v7x, 32 devices: a whole 2x2x4 slice. The times are simulated.
32 devices in a mesh: vblk: 8 (over y, x, core), pair: 4 (over z).
Axes of the slice: x: 2, y: 2, z: 4, core: 2. Of those that a mesh axis runs over, the one named last changes fastest.
Arguments:
- amplitudes: bfloat16 [128, 384, 384], P(('vblk', 'pair')), may hold values from -6 to 6
- domain_mask: int32 [128, 3], P(('vblk', 'pair')), may hold values from 0 to 1, as said below
- centers: int32 [128], P(('vblk', 'pair')), may hold values from 0 to 7, as said below
- chol_panel: bfloat16 [8, 8, 5, 128, 128], P('vblk', None, None, 'pair'), may hold values from -0.3125 to 0.3125
Outputs:
- residual_tiles: float32 [128, 384, 384], P(('vblk', 'pair'))
Inputs may be any that keep to these rules, and one draw needn't show every extreme that they name: centers[p] differs from p // 16 (the block of the region that holds pair p) by at most 1, and by exactly 1 in both directions for some pairs. `domain_mask`: the middle column of the window (column 1 for a window of 3 blocks) is 1 for every pair; column k is 0 where the window block centers + k minus the middle index lies outside 0 to 7.
All inputs are finite; a program needn't handle non-finite values.
Results may differ from a plain program's by a relative error of at most 0.0029.
Values may be sent and summed in bfloat16 or wider, within the bound.
No kernel may reach another device: no remote copies, remote signals or barrier semaphores. Data moves between devices by JAX's collectives and lax.ppermute only.
A program may use at most 128 MiB of HBM per device.

v0:
```python
import jax
import jax.numpy as jnp
from jax import lax
from jax.sharding import PartitionSpec as P

VB = 128
DW = 3
RCH = 1


def from_behind(value, axis, steps):
    count = lax.axis_size(axis)
    first, last = (max(0, -steps), min(count, count - steps))
    return lax.ppermute(value, axis, [(source, source + steps) for source in range(first, last)])


def assemble(window):
    strips = []
    for a in range(DW):
        strips.append(
            jnp.concatenate([window[..., a, :, b - a + DW - 1, :, :] for b in range(DW)], axis=-1)
        )
    return jnp.concatenate(strips, axis=-2)


def local(amplitudes, domain_mask, centers, chol_panel):
    halfwidth = (DW - 1) // 2
    furthest = RCH + halfwidth
    whole = lax.all_gather(chol_panel, "pair", axis=3, tiled=True)
    nearby = []
    for distance in range(-furthest, furthest + 1):
        if distance == 0:
            nearby.append(whole)
        else:
            nearby.append(from_behind(whole, "vblk", -distance))
    neighbourhood = jnp.concatenate(nearby, axis=0)
    position = lax.axis_index("vblk")
    offset = centers - position + furthest - halfwidth
    row_index = offset[:, None] + jnp.arange(DW, dtype=jnp.int32)[None, :]
    window = jnp.take(neighbourhood, row_index, axis=0)
    blocks = assemble(window)
    live_cols = jnp.repeat(domain_mask, VB, axis=1) > 0
    keep_tile = live_cols[:, :, None] & live_cols[:, None, :]
    masked = jnp.where(keep_tile, amplitudes, jnp.zeros_like(amplitudes))
    half_product = jnp.einsum(
        "pqij,pjk->pqik", blocks, masked, preferred_element_type=jnp.float32
    ).astype(jnp.bfloat16)
    ladder = jnp.einsum("pqik,pqlk->pil", half_product, blocks, preferred_element_type=jnp.float32)
    return jnp.where(keep_tile, ladder, jnp.zeros_like(ladder))


def solution(mesh):
    return jax.shard_map(
        local,
        mesh=mesh,
        in_specs=(
            P(("vblk", "pair"), None, None),
            P(("vblk", "pair"), None),
            P(("vblk", "pair")),
            P("vblk", None, None, "pair", None),
        ),
        out_specs=P(("vblk", "pair"), None, None),
        check_vma=False,
    )
```

profile of v0, /device:TPU:0, one launch (start us, length us, event | category | flops | bytes accessed | tf_op | source)
XLA Modules:
  0.0 181.5 jit_solution(7642532700543118598)
XLA Ops:
  6.5 0.0 all-gather.2.cloned.1.call-start
  6.5 0.7 all-gather.2.cloned.1.call-update
  7.3 37.1 %all-gather.2.cloned.1.call-done = bf16[1,8,5,128,128]{4,3,2,1,0:T(8,128)(2,1)} async-done(((bf16[1,8,5,32,128]{4,3,2,1,0:T(8,128)(2,1)}), bf16[1,8,5,128,128]{4,3,2,1,0:T(8,128)(2,1)}) %all-gather.2.cloned.1.call-update) | async-done | bytes 1310736 | tf_op jit(solution)/shard_map/all_gather | solution.py:29
  44.4 3.4 %collective-permute-start = (bf16[1,8,5,128,128]{4,3,2,1,0:T(8,128)(2,1)}, bf16[1,8,5,128,128]{4,3,2,1,0:T(8,128)(2,1)S(1)}, u32[]{:S(2)}, u32[]{:S(2)}) collective-permute-start(bf16[1,8,5,128,128]{4,3,2,1,0:T(8,128)(2,1)} %all-gather.2.cloned.1.call-done), channel_id=1, source_target_pairs={{0,8},{4,12},{8,16},{12,20},{16,24},{20,28},{1,9},{5,13},{9,17},{1... | collective-permute-start | bytes 3932168 | tf_op jit(solution)/shard_map/ppermute | solution.py:14
  47.8 2.4 %collective-permute-start.1 = (bf16[1,8,5,128,128]{4,3,2,1,0:T(8,128)(2,1)}, bf16[1,8,5,128,128]{4,3,2,1,0:T(8,128)(2,1)}, u32[]{:S(2)}, u32[]{:S(2)}) collective-permute-start(bf16[1,8,5,128,128]{4,3,2,1,0:T(8,128)(2,1)} %all-gather.2.cloned.1.call-done), channel_id=1, source_target_pairs={{0,4},{4,8},{8,12},{12,16},{16,20},{20,24},{24,28},{1,5},{5,9},{9,... | collective-permute-start | bytes 3932168 | tf_op jit(solution)/shard_map/ppermute | solution.py:14
  50.2 0.7 subtract_add_fusion
  50.8 1.3 collective-permute-start.2
  52.1 0.1 compare_select_fusion
  52.2 0.1 reshape.71
  52.3 1.3 collective-permute-start.3
  53.6 0.1 fusion.17
  53.6 0.1 copy.7
  53.8 0.7 broadcast_compare_fusion
  54.4 0.1 copy.6
  54.6 0.1 broadcast_bitcast_fusion
  54.6 22.6 %collective-permute-done = bf16[1,8,5,128,128]{4,3,2,1,0:T(8,128)(2,1)S(1)} collective-permute-done((bf16[1,8,5,128,128]{4,3,2,1,0:T(8,128)(2,1)}, bf16[1,8,5,128,128]{4,3,2,1,0:T(8,128)(2,1)S(1)}, u32[]{:S(2)}, u32[]{:S(2)}) %collective-permute-start) | collective-permute-done | bytes 1310752 | tf_op jit(solution)/shard_map/ppermute | solution.py:14
  77.3 1.2 constant_dynamic-update-slice_fusion.4
  78.4 0.0 collective-permute-done.1
  78.4 2.5 %constant_dynamic-update-slice_fusion.3 = bf16[5,8,5,128,128]{4,3,2,1,0:T(8,128)(2,1)} fusion(bf16[5,8,5,128,128]{4,3,2,1,0:T(8,128)(2,1)} %constant_dynamic-update-slice_fusion.4, bf16[1,8,5,128,128]{4,3,2,1,0:T(8,128)(2,1)} %collective-permute-done.1), kind=kLoop, calls=%fused_computation.24 | loop fusion | bytes 2621440
  81.0 2.5 %constant_dynamic-update-slice_fusion.2 = bf16[5,8,5,128,128]{4,3,2,1,0:T(8,128)(2,1)} fusion(bf16[5,8,5,128,128]{4,3,2,1,0:T(8,128)(2,1)} %constant_dynamic-update-slice_fusion.3, bf16[1,8,5,128,128]{4,3,2,1,0:T(8,128)(2,1)} %all-gather.2.cloned.1.call-done), kind=kLoop, calls=%fused_computation.23 | loop fusion | bytes 2621440
  83.5 0.0 collective-permute-done.2
  83.5 1.1 constant_dynamic-update-slice_fusion.1
  84.6 48.8 %collective-permute-done.3 = bf16[1,8,5,128,128]{4,3,2,1,0:T(8,128)(2,1)} collective-permute-done((bf16[1,8,5,128,128]{4,3,2,1,0:T(8,128)(2,1)}, bf16[1,8,5,128,128]{4,3,2,1,0:T(8,128)(2,1)}, u32[]{:S(2)}, u32[]{:S(2)}) %collective-permute-start.3) | collective-permute-done | bytes 1310752 | tf_op jit(solution)/shard_map/ppermute | solution.py:14
  133.5 2.6 %constant_dynamic-update-slice_fusion = bf16[5,8,5,128,128]{4,3,2,1,0:T(8,128)(2,1)} fusion(bf16[5,8,5,128,128]{4,3,2,1,0:T(8,128)(2,1)} %constant_dynamic-update-slice_fusion.1, bf16[1,8,5,128,128]{4,3,2,1,0:T(8,128)(2,1)} %collective-permute-done.3), kind=kLoop, calls=%fused_computation.21 | loop fusion | bytes 2621440 | tf_op jit(solution)/shard_map/concatenate | solution.py:36
  136.0 10.0 %gather_fusion = bf16[12,8,5,128,128]{4,3,2,1,0:T(8,128)(2,1)} fusion(bf16[5,8,5,128,128]{4,3,2,1,0:T(8,128)(2,1)} %constant_dynamic-update-slice_fusion, s32[1024]{0:T(1024)S(1)} %pad_clamp_fusion), kind=kCustom, calls=%fused_computation | custom fusion | bytes 31457328 | tf_op jit(solution)/shard_map/jit(_take)/gather | solution.py:40
  146.0 8.3 %copy_select_fusion = bf16[4,3,8,5,128,128]{5,4,2,0,3,1:T(8,128)(2,1)S(1)} fusion(bf16[4,3,8,5,128,128]{5,4,3,2,1,0:T(8,128)(2,1)} %bitcast.39, pred[4,3]{0,1:T(4,128)(4,1)S(1)} %copy.7), kind=kLoop, calls=%fused_computation.1 | loop fusion | flops 7864320 | bytes 31457292 | tf_op jit(solution)/shard_map/jit(_take)/select_n | solution.py:40
  154.3 0.0 copy-start
  154.3 3.3 %slice_bitcast_fusion.8 = (bf16[4,8,128,128]{3,2,1,0:T(8,128)(2,1)S(1)}, bf16[4,8,128,128]{3,2,1,0:T(8,128)(2,1)S(1)}, bf16[4,8,128,128]{3,2,1,0:T(8,128)(2,1)S(...) fusion(bf16[4,3,8,5,128,128]{5,4,2,0,3,1:T(8,128)(2,1)S(1)} %co, ...), kind=kLoop, calls=%fused_computation.19 | loop fusion | bytes 18874368 | tf_op jit(solution)/shard_map/squeeze | solution.py:21
  157.7 0.0 copy-done
  157.7 8.3 %fusion.29 = bf16[4,8,384,384]{3,2,1,0:T(8,128)(2,1)} fusion(bf16[4,8,128,128]{3,2,1,0:T(8,128)(2,1)S(1)} %get-tuple-element.6, bf16[4,8,128,128]{3,2,1,0:T(8,128)(2,1)S(1)} %get-tuple-element.7, bf16[4,8,128,128]{3,2,1,0:T(8,128)(2,1)S(1)} %get-tuple-element.8, bf16[4,8,128,128]{3,2,1,0:T(8,128)(2,1)S(1)} %get-tuple-element.9, ...), kind=kOutput, calls=%fused_computation.4.clone.clone.clone.2 | convolution fusion | flops 3714711552 | bytes 20055552 | tf_op jit(solution)/shard_map/pqij,pjk->pqik/dot_general | solution.py:45
  165.9 8.7 %and_select_fusion = f32[4,384,384]{2,1,0:T(8,128)} fusion(bf16[4,8,128,128]{3,2,1,0:T(8,128)(2,1)S(1)} %get-tuple-element.6, bf16[4,8,128,128]{3,2,1,0:T(8,128)(2,1)S(1)} %get-tuple-element.7, bf16[4,8,128,128]{3,2,1,0:T(8,128)(2,1)S(1)} %get-tuple-element.8, bf16[4,8,128,128]{3,2,1,0:T(8,128)(2,1)S(1)} %get-tuple-element.9, ...), kind=kOutput, calls=%fused_computation.6 | convolution fusion | flops 3709992960 | bytes 21235200 | tf_op jit(solution)/shard_map/pqik,pqlk->pil/dot_general | solution.py:48
  (1 shorter events, 0.0 us)
Async XLA Ops:
  6.5 37.8 %all-gather.2.cloned.1.call-start = ((), (), s32[]{:S(2)}) async-start(), calls=%async_computation | async-start | bytes 1638400 | tf_op jit(solution)/shard_map/all_gather | solution.py:29
  44.4 32.9 %collective-permute-start = (bf16[1,8,5,128,128]{4,3,2,1,0:T(8,128)(2,1)}, bf16[1,8,5,128,128]{4,3,2,1,0:T(8,128)(2,1)S(1)}, u32[]{:S(2)}, u32[]{:S(2)}) collective-permute-start(bf16[1,8,5,128,128]{4,3,2,1,0:T(8,128)(2,1)} %all-gather.2.cloned.1.call-done), channel_id=1, source_target_pairs={{0,8},{4,12},{8,16},{12,20},{16,24},{20,28},{1,9},{5,13},{9,17},{1... | collective-permute-start | bytes 3932168 | tf_op jit(solution)/shard_map/ppermute | solution.py:14
  47.8 30.6 %collective-permute-start.1 = (bf16[1,8,5,128,128]{4,3,2,1,0:T(8,128)(2,1)}, bf16[1,8,5,128,128]{4,3,2,1,0:T(8,128)(2,1)}, u32[]{:S(2)}, u32[]{:S(2)}) collective-permute-start(bf16[1,8,5,128,128]{4,3,2,1,0:T(8,128)(2,1)} %all-gather.2.cloned.1.call-done), channel_id=1, source_target_pairs={{0,4},{4,8},{8,12},{12,16},{16,20},{20,24},{24,28},{1,5},{5,9},{9,... | collective-permute-start | bytes 3932168 | tf_op jit(solution)/shard_map/ppermute | solution.py:14
  50.8 32.6 %collective-permute-start.2 = (bf16[1,8,5,128,128]{4,3,2,1,0:T(8,128)(2,1)}, bf16[1,8,5,128,128]{4,3,2,1,0:T(8,128)(2,1)S(1)}, u32[]{:S(2)}, u32[]{:S(2)}) collective-permute-start(bf16[1,8,5,128,128]{4,3,2,1,0:T(8,128)(2,1)} %all-gather.2.cloned.1.call-done), channel_id=1, source_target_pairs={{4,0},{8,4},{12,8},{16,12},{20,16},{24,20},{28,24},{5,1},{9,5},{13... | collective-permute-start | bytes 3932168 | tf_op jit(solution)/shard_map/ppermute | solution.py:14
  52.3 81.2 %collective-permute-start.3 = (bf16[1,8,5,128,128]{4,3,2,1,0:T(8,128)(2,1)}, bf16[1,8,5,128,128]{4,3,2,1,0:T(8,128)(2,1)}, u32[]{:S(2)}, u32[]{:S(2)}) collective-permute-start(bf16[1,8,5,128,128]{4,3,2,1,0:T(8,128)(2,1)} %all-gather.2.cloned.1.call-done), channel_id=1, source_target_pairs={{8,0},{12,4},{16,8},{20,12},{24,16},{28,20},{9,1},{13,5},{17,9},{2... | collective-permute-start | bytes 3932168 | tf_op jit(solution)/shard_map/ppermute | solution.py:14
  154.3 3.4 %copy-start = (bf16[4,384,384]{2,1,0:T(8,128)(2,1)S(1)}, bf16[4,384,384]{2,1,0:T(8,128)(2,1)}, u32[]{:S(2)}) copy-start(bf16[4,384,384]{2,1,0:T(8,128)(2,1)} %param.4) | copy-start | bytes 3538948
Sparse Core Ops, SparseCore 0:
  8.9 35.3 all-gather.1
where the time goes:
time: 182 us
  waiting for transfers between devices  109 us (60%)
  local copies, waits for them, and re-layouts  23.7 us (13%)
  matrix products  17 us (9%)
  between operations  13.5 us (7%)
  other arithmetic  9.76 us (5%)
  starting transfers between devices  8.37 us (5%)
    ppermute x4, waiting for transfers between devices, from_behind(): lax.ppermute(value, axis, [(source, source + steps) for source in range(f...  71.4 us
    all_gather x1, waiting for transfers between devices, local(): whole = lax.all_gather(chol_panel, 'pair', axis=3, tiled=True)  37.1 us
    gather x1, local copies, waits for them, and re-layouts, local(): window = jnp.take(neighbourhood, row_index, axis=0)  10 us
    dot_general x1, matrix products, local(): jnp.einsum('pqik,pqlk->pil', half_product, blocks, preferred_element_type...  8.71 us
    ppermute x4, starting transfers between devices, from_behind(): lax.ppermute(value, axis, [(source, source + steps) for source in range(f...  8.37 us
    select_n x2, other arithmetic, local(): window = jnp.take(neighbourhood, row_index, axis=0)  8.33 us
    dot_general x1, matrix products, local(): jnp.einsum('pqij,pjk->pqik', blocks, masked, preferred_element_type=jnp.f...  8.28 us
    unnamed x6, local copies, waits for them, and re-layouts  7.38 us
  transfers between devices with their start and end apart: 5, of which 3 were waited for; matrix products, arithmetic and copies ran while one was open for 5% of the time, Pallas kernels for 0%

commit v1 on v0

v1 whole, which is shorter than its diff:
```python
import functools

import jax
import jax.numpy as jnp
from jax import lax
from jax.experimental import pallas as pl
from jax.experimental.pallas import tpu as pltpu
from jax.sharding import PartitionSpec as P

VB = 128
DW = 3
CHUNKS = (2, 2, 2, 2)
AXES = ("vblk", "pair")


def ladder_kernel(chunk, has_sum, *refs):
    if has_sum:
        rel_ref, live_ref, where_ref, amp_ref, *panels, sum_ref, out_ref, tiles, strips, halves, sem = refs
    else:
        rel_ref, live_ref, where_ref, amp_ref, *panels, out_ref, tiles, strips, halves, sem = refs
    shards = panels[0].shape[0]
    rows = panels[0].shape[3]
    npair = amp_ref.shape[0]

    def copy(i, s):
        at = where_ref[0, i]
        row = pl.multiple_of(where_ref[1, s] * rows, rows)
        return pltpu.make_async_copy(
            panels[i].at[s], tiles.at[at, :, :, pl.ds(row, rows), :], sem.at[i, s]
        )

    for i in range(len(panels)):
        for s in range(shards):
            copy(i, s).start()
    for i in range(len(panels)):
        for s in range(shards):
            copy(i, s).wait()

    @pl.loop(0, npair)
    def _(p):
        rel = rel_ref[p]
        live = [live_ref[p, k] > 0 for k in range(DW)]
        masked = jnp.concatenate(
            [
                jnp.concatenate(
                    [
                        jnp.where(live[a] & live[b], amp_ref[p, pl.ds(a * VB, VB), pl.ds(b * VB, VB)], 0)
                        for b in range(DW)
                    ],
                    axis=1,
                )
                for a in range(DW)
            ],
            axis=0,
        ).astype(jnp.bfloat16)
        for q in range(chunk):
            for a in range(DW):
                strips[pl.ds(a * VB, VB), pl.ds(q * DW * VB, DW * VB)] = jnp.concatenate(
                    [tiles[rel + a, q, b - a + DW - 1] for b in range(DW)], axis=1
                )
        for q in range(chunk):
            cols = pl.ds(q * DW * VB, DW * VB)
            halves[:, cols] = jnp.dot(
                strips[:, cols], masked, preferred_element_type=jnp.float32
            ).astype(jnp.bfloat16)
        ladder = lax.dot_general(
            halves[...], strips[...], (((1,), (1,)), ((), ())), preferred_element_type=jnp.float32
        )
        for a in range(DW):
            for b in range(DW):
                at = (p, pl.ds(a * VB, VB), pl.ds(b * VB, VB))
                part = ladder[a * VB : (a + 1) * VB, b * VB : (b + 1) * VB]
                if has_sum:
                    part = part + sum_ref[at]
                out_ref[at] = jnp.where(live[a] & live[b], part, 0.0)


def ladder(chunk, rel, live, where, amplitudes, panels, total):
    npair, width, _ = amplitudes.shape
    vmem = pl.BlockSpec(memory_space=pltpu.VMEM)
    smem = pl.BlockSpec(memory_space=pltpu.SMEM)
    anyspace = pl.BlockSpec(memory_space=pl.ANY)
    shards, _, offs, rows, vb = panels[0].shape
    sums = [] if total is None else [total]
    flops = npair * chunk * 4 * width**3
    return pl.pallas_call(
        functools.partial(ladder_kernel, chunk, bool(sums)),
        out_shape=jax.ShapeDtypeStruct((npair, width, width), jnp.float32),
        in_specs=[smem, smem, smem, vmem] + [anyspace] * len(panels) + [vmem] * len(sums),
        out_specs=vmem,
        scratch_shapes=[
            pltpu.VMEM((2 * DW, chunk, offs, shards * rows, vb), jnp.bfloat16),
            pltpu.VMEM((width, chunk * width), jnp.bfloat16),
            pltpu.VMEM((width, chunk * width), jnp.bfloat16),
            pltpu.SemaphoreType.DMA((len(panels), shards)),
        ],
        cost_estimate=pl.CostEstimate(flops=flops, bytes_accessed=6 << 20, transcendentals=0),
    )(rel, live, where, amplitudes, *panels, *sums)


def solution(mesh):
    nv, nz = mesh.shape["vblk"], mesh.shape["pair"]
    chips = nv // 2

    def moves(step):
        pairs = []
        for v in range(nv):
            for z in range(nz):
                to = step(v // 2, v % 2, z)
                if to is not None and 0 <= to[0] < chips:
                    pairs.append((v * nz + z, (to[0] * 2 + to[1]) * nz + to[2]))
        return pairs

    sideways = [moves(lambda i, c, z, s=s: (i, c, z ^ s)) for s in range(1, nz)]
    neighbour = moves(lambda i, c, z: (i ^ 1, c, z))
    relay = moves(lambda i, c, z: (i - 2 if i % 2 else i + 2, c, z))
    sibling = moves(lambda i, c, z: (i, 1 - c, z))

    def local(amplitudes, domain_mask, centers, chol_panel):
        v = lax.axis_index("vblk")
        z = lax.axis_index("pair")
        chip, core = v // 2, v % 2
        odd = chip % 2
        rel = centers - v + 1
        unused = 2 * DW - 1
        near = jnp.where(core == 0, 1, 3)
        use_nb = core != odd
        places = jnp.stack(
            [
                2 + 0 * v,
                jnp.where(odd == 1, 0, 4),
                jnp.where(odd == 1, 4, 0),
                jnp.where(core == 0, 3, 1),
                jnp.where(use_nb, near, unused),
                jnp.where(use_nb, unused, near),
            ]
        )
        slots = z ^ jnp.arange(6, dtype=jnp.int32)
        where = jnp.stack([places, slots]).astype(jnp.int32)
        total = None
        start = 0
        for chunk in CHUNKS:
            own = chol_panel[0, start : start + chunk]
            start += chunk
            gathered = jnp.stack([own] + [lax.ppermute(own, AXES, m) for m in sideways])
            swapped = lax.ppermute(gathered, AXES, neighbour)
            relayed = lax.ppermute(swapped, AXES, relay)
            mine = [gathered, swapped, relayed]
            panels = mine + [lax.ppermute(x, AXES, sibling) for x in mine]
            total = ladder(chunk, rel, domain_mask, where, amplitudes, panels, total)
        return total

    return jax.shard_map(
        local,
        mesh=mesh,
        in_specs=(
            P(AXES, None, None),
            P(AXES, None),
            P(AXES),
            P("vblk", None, None, "pair", None),
        ),
        out_specs=P(AXES, None, None),
        check_vma=False,
    )
```

time: 182 us -> 104 us (0.57)
  waiting for transfers between devices: 109 us -> 25.5 us
  Pallas kernels: 0 us -> 33.8 us
  starting transfers between devices: 8.37 us -> 39.9 us
  local copies, waits for them, and re-layouts: 23.7 us -> 2.79 us
  matrix products: 17 us -> 0 us
  between operations: 13.5 us -> 0.39 us
  other arithmetic: 9.76 us -> 1.35 us
    ppermute x4 -> x32, waiting for transfers between devices: 71.4 us -> 25.5 us  [the longest x12 10.6 us: local(): gathered = jnp.stack([own] + [lax.ppermute(own, AXES, m) for m in sideways])]
    all_gather x1 -> x0, waiting for transfers between devices: 37.1 us -> none  [local(): whole = lax.all_gather(chol_panel, 'pair', axis=3, tiled=True)]
    pallas_call x0 -> x4, Pallas kernels: none -> 33.8 us  [ladder(): pl.pallas_call(functools.partial(ladder_kernel, chunk, bool(sums)), out_s...]
    ppermute x4 -> x32, starting transfers between devices: 8.37 us -> 39.9 us  [the longest x12 22 us: local(): gathered = jnp.stack([own] + [lax.ppermute(own, AXES, m) for m in sideways])]
    dot_general x2 -> x0, matrix products: 17 us -> none  [the longest x1 8.71 us: local(): jnp.einsum('pqik,pqlk->pil', half_product, blocks, preferred_element_type...]
    gather x1 -> x0, local copies, waits for them, and re-layouts: 10 us -> none  [local(): window = jnp.take(neighbourhood, row_index, axis=0)]
    select_n x2 -> x0, other arithmetic: 8.33 us -> none  [local(): window = jnp.take(neighbourhood, row_index, axis=0)]
    unnamed x6 -> x32, local copies, waits for them, and re-layouts: 7.38 us -> 1.6 us
  transfers between devices with their start and end apart: 5 -> 32, of which waited for: 3 -> 10; matrix products, arithmetic and copies ran while one was open for 5% -> 1% of each run, Pallas kernels for 0% -> 24%
where the time goes in v1:
time: 104 us
  starting transfers between devices  39.9 us (38%)
  Pallas kernels  33.8 us (32%)
  waiting for transfers between devices  25.5 us (25%)
  local copies, waits for them, and re-layouts  2.79 us (3%)
  other arithmetic  1.35 us (1%)
    pallas_call x4, Pallas kernels, ladder(): pl.pallas_call(functools.partial(ladder_kernel, chunk, bool(sums)), out_s...  33.8 us
    ppermute x12, starting transfers between devices, local(): gathered = jnp.stack([own] + [lax.ppermute(own, AXES, m) for m in sideways])  22 us
    ppermute x4, starting transfers between devices, local(): relayed = lax.ppermute(swapped, AXES, relay)  13 us
    ppermute x12, waiting for transfers between devices, local(): gathered = jnp.stack([own] + [lax.ppermute(own, AXES, m) for m in sideways])  10.6 us
    ppermute x4, waiting for transfers between devices, local(): relayed = lax.ppermute(swapped, AXES, relay)  7.76 us
    ppermute x4, waiting for transfers between devices, local(): swapped = lax.ppermute(gathered, AXES, neighbour)  7.09 us
    ppermute x4, starting transfers between devices, local(): swapped = lax.ppermute(gathered, AXES, neighbour)  3.59 us
  transfers between devices with their start and end apart: 32, of which 10 were waited for; matrix products, arithmetic and copies ran while one was open for 1% of the time, Pallas kernels for 24%

profile of v1, /device:TPU:0, one launch (start us, length us, event | category | flops | bytes accessed | tf_op | source)
XLA Modules:
  0.0 103.8 jit_solution(17129921585694584711)
XLA Ops:
  0.0 1.1 %fusion = (bf16[1,2,5,32,128]{4,3,2,1,0:T(8,128)(2,1)S(1)}, bf16[2,5,32,128]{3,2,1,0:T(8,128)(2,1)S(1)}, bf16[2,5,32,128]{3,2,1,0:T(8,128)(2,1)S(1)}, bf16[2,5,3...) fusion(bf16[1,8,5,32,128]{4,3,2,1,0:T(8,128)(2,1)} %param.7), kind=kLoop, calls=%fused_computation.11 | loop fusion | bytes 983040 | tf_op jit(solution)/shard_map/slice | solution.py:143
  1.1 3.1 %collective-permute-start.24 = (bf16[2,5,32,128]{3,2,1,0:T(8,128)(2,1)S(1)}, bf16[2,5,32,128]{3,2,1,0:T(8,128)(2,1)S(1)}, u32[]{:S(2)}, u32[]{:S(2)}) collective-permute-start(bf16[2,5,32,128]{3,2,1,0:T(8,128)(2,1)S(1)} %get-tuple-element.9), channel_id=1, source_target_pairs={{0,1},{1,0},{2,3},{3,2},{4,5},{5,4},{6,7},{7,6},{8,9},{9,8},{10,11... | collective-permute-start | bytes 245768 | tf_op jit(solution)/shard_map/ppermute | solution.py:145
  4.2 2.6 %collective-permute-start.25 = (bf16[2,5,32,128]{3,2,1,0:T(8,128)(2,1)S(1)}, bf16[2,5,32,128]{3,2,1,0:T(8,128)(2,1)S(1)}, u32[]{:S(2)}, u32[]{:S(2)}) collective-permute-start(bf16[2,5,32,128]{3,2,1,0:T(8,128)(2,1)S(1)} %get-tuple-element.9), channel_id=1, source_target_pairs={{0,2},{1,3},{2,0},{3,1},{4,6},{5,7},{6,4},{7,5},{8,10},{9,11},{10,... | collective-permute-start | bytes 245768 | tf_op jit(solution)/shard_map/ppermute | solution.py:145
  6.8 0.9 collective-permute-start.16
  7.7 3.5 %collective-permute-start.17 = (bf16[2,5,32,128]{3,2,1,0:T(8,128)(2,1)S(1)}, bf16[2,5,32,128]{3,2,1,0:T(8,128)(2,1)S(1)}, u32[]{:S(2)}, u32[]{:S(2)}) collective-permute-start(bf16[2,5,32,128]{3,2,1,0:T(8,128)(2,1)S(1)} %get-tuple-element.8), channel_id=1, source_target_pairs={{0,2},{1,3},{2,0},{3,1},{4,6},{5,7},{6,4},{7,5},{8,10},{9,11},{10,... | collective-permute-start | bytes 245768 | tf_op jit(solution)/shard_map/ppermute | solution.py:145
  11.2 0.0 collective-permute-done.24
  11.2 0.3 collective-permute-start.18
  11.5 3.0 %collective-permute-done.25 = bf16[2,5,32,128]{3,2,1,0:T(8,128)(2,1)S(1)} collective-permute-done((bf16[2,5,32,128]{3,2,1,0:T(8,128)(2,1)S(1)}, bf16[2,5,32,128]{3,2,1,0:T(8,128)(2,1)S(1)}, u32[]{:S(2)}, u32[]{:S(2)}) %collective-permute-start.25) | collective-permute-done | bytes 81952 | tf_op jit(solution)/shard_map/ppermute | solution.py:145
  14.5 0.0 collective-permute-start.8
  14.5 0.0 collective-permute-done.26
  14.5 7.8 %collective-permute-start.9 = (bf16[2,5,32,128]{3,2,1,0:T(8,128)(2,1)S(1)}, bf16[2,5,32,128]{3,2,1,0:T(8,128)(2,1)S(1)}, u32[]{:S(2)}, u32[]{:S(2)}) collective-permute-start(bf16[2,5,32,128]{3,2,1,0:T(8,128)(2,1)S(1)} %get-tuple-element.7), channel_id=1, source_target_pairs={{0,2},{1,3},{2,0},{3,1},{4,6},{5,7},{6,4},{7,5},{8,10},{9,11},{10,... | collective-permute-start | bytes 245768 | tf_op jit(solution)/shard_map/ppermute | solution.py:145
  22.3 0.0 collective-permute-done.16
  22.3 0.3 collective-permute-start.10
  22.7 0.0 collective-permute-done.17
  22.7 1.5 %collective-permute-start.27 = (bf16[4,2,5,32,128]{4,3,2,1,0:T(8,128)(2,1)S(1)}, bf16[4,2,5,32,128]{4,3,2,1,0:T(8,128)(2,1)}, u32[]{:S(2)}, u32[]{:S(2)}) collective-permute-start(bf16[4,2,5,32,128]{4,3,2,1,0:T(8,128)(2,1)S(1)} %pad_maximum_fusion.3.refs_4_), channel_id=1, source_target_pairs={{0,8},{1,9},{2,10},{3,11},{4,12},{5,13},{6,14},{7,15},{8,0},{9,1},... | collective-permute-start | bytes 983048 | tf_op jit(solution)/shard_map/ppermute | solution.py:146
  24.2 0.0 collective-permute-done.18
  24.2 0.0 collective-permute-start.29
  24.3 0.0 collective-permute-done.8
  24.3 0.5 collective-permute-start
  24.7 1.8 %collective-permute-done.9 = bf16[2,5,32,128]{3,2,1,0:T(8,128)(2,1)S(1)} collective-permute-done((bf16[2,5,32,128]{3,2,1,0:T(8,128)(2,1)S(1)}, bf16[2,5,32,128]{3,2,1,0:T(8,128)(2,1)S(1)}, u32[]{:S(2)}, u32[]{:S(2)}) %collective-permute-start.9) | collective-permute-done | bytes 81952 | tf_op jit(solution)/shard_map/ppermute | solution.py:145
  26.6 1.9 %collective-permute-start.1 = (bf16[2,5,32,128]{3,2,1,0:T(8,128)(2,1)S(1)}, bf16[2,5,32,128]{3,2,1,0:T(8,128)(2,1)S(1)}, u32[]{:S(2)}, u32[]{:S(2)}) collective-permute-start(bf16[2,5,32,128]{3,2,1,0:T(8,128)(2,1)S(1)} %get-tuple-element.6), channel_id=1, source_target_pairs={{0,2},{1,3},{2,0},{3,1},{4,6},{5,7},{6,4},{7,5},{8,10},{9,11},{10,... | collective-permute-start | bytes 245768 | tf_op jit(solution)/shard_map/ppermute | solution.py:145
  28.4 0.3 collective-permute-done.10
  28.8 1.2 %collective-permute-start.2 = (bf16[2,5,32,128]{3,2,1,0:T(8,128)(2,1)S(1)}, bf16[2,5,32,128]{3,2,1,0:T(8,128)(2,1)S(1)}, u32[]{:S(2)}, u32[]{:S(2)}) collective-permute-start(bf16[2,5,32,128]{3,2,1,0:T(8,128)(2,1)S(1)} %get-tuple-element.6), channel_id=1, source_target_pairs={{0,3},{1,2},{2,1},{3,0},{4,7},{5,6},{6,5},{7,4},{8,11},{9,10},{10,... | collective-permute-start | bytes 245768 | tf_op jit(solution)/shard_map/ppermute | solution.py:145
  30.0 1.0 collective-permute-done
  30.9 0.6 collective-permute-start.19
  31.6 4.5 %collective-permute-done.1 = bf16[2,5,32,128]{3,2,1,0:T(8,128)(2,1)S(1)} collective-permute-done((bf16[2,5,32,128]{3,2,1,0:T(8,128)(2,1)S(1)}, bf16[2,5,32,128]{3,2,1,0:T(8,128)(2,1)S(1)}, u32[]{:S(2)}, u32[]{:S(2)}) %collective-permute-start.1) | collective-permute-done | bytes 81952 | tf_op jit(solution)/shard_map/ppermute | solution.py:145
  36.1 0.0 collective-permute-start.21
  36.1 0.0 collective-permute-done.2
  36.1 0.7 collective-permute-start.11
  36.8 0.0 collective-permute-done.27.refs_5_
  36.8 0.0 collective-permute-start.13
  36.8 0.0 collective-permute-done.29.refs_7_
  36.8 4.2 %collective-permute-start.28 = (bf16[4,2,5,32,128]{4,3,2,1,0:T(8,128)(2,1)}, bf16[4,2,5,32,128]{4,3,2,1,0:T(8,128)(2,1)}, u32[]{:S(2)}, u32[]{:S(2)}) collective-permute-start(bf16[4,2,5,32,128]{4,3,2,1,0:T(8,128)(2,1)} %collective-permute-done.27.refs_5_), channel_id=1, source_target_pairs={{0,16},{1,17},{2,18},{3,19},{4,20},{5,21},{6,22},{7,23},{24,8},{25... | collective-permute-start | bytes 983048 | tf_op jit(solution)/shard_map/ppermute | solution.py:147
  41.0 0.4 collective-permute-done.19.refs_5_
  41.4 0.8 collective-permute-start.3
  42.2 0.0 collective-permute-done.21.refs_7_
  42.2 0.0 collective-permute-start.30
  42.2 6.2 %collective-permute-done.11.refs_5_ = bf16[4,2,5,32,128]{4,3,2,1,0:T(8,128)(2,1)S(1)} collective-permute-done((bf16[4,2,5,32,128]{4,3,2,1,0:T(8,128)(2,1)S(1)}, bf16[4,2,5,32,128]{4,3,2,1,0:T(8,128)(2,1)S(1)}, u32[]{:S(2)}, u32[]{:S(2)}) %collective-permute-start.11) | collective-permute-done | bytes 327712 | tf_op jit(solution)/shard_map/ppermute | solution.py:146
  48.4 3.4 %collective-permute-start.20 = (bf16[4,2,5,32,128]{4,3,2,1,0:T(8,128)(2,1)S(1)}, bf16[4,2,5,32,128]{4,3,2,1,0:T(8,128)(2,1)S(1)}, u32[]{:S(2)}, u32[]{:S(2)}) collective-permute-start(bf16[4,2,5,32,128]{4,3,2,1,0:T(8,128)(2,1)S(1)} %collective-permute-done.19.refs_5_), channel_id=1, source_target_pairs={{0,16},{1,17},{2,18},{3,19},{4,20},{5,21},{6,22},{7,23},{24,8},{25... | collective-permute-start | bytes 983048 | tf_op jit(solution)/shard_map/ppermute | solution.py:147
  51.9 1.3 %collective-permute-start.12 = (bf16[4,2,5,32,128]{4,3,2,1,0:T(8,128)(2,1)S(1)}, bf16[4,2,5,32,128]{4,3,2,1,0:T(8,128)(2,1)S(1)}, u32[]{:S(2)}, u32[]{:S(2)}) collective-permute-start(bf16[4,2,5,32,128]{4,3,2,1,0:T(8,128)(2,1)S(1)} %collective-permute-done.11.refs_5_), channel_id=1, source_target_pairs={{0,16},{1,17},{2,18},{3,19},{4,20},{5,21},{6,22},{7,23},{24,8},{25... | collective-permute-start | bytes 983048 | tf_op jit(solution)/shard_map/ppermute | solution.py:147
  53.2 0.1 collective-permute-start.31
  53.3 0.6 subtract_add_fusion.refs_0_
  53.9 0.5 collective-permute-done.3.refs_5_
  54.4 0.0 collective-permute-start.22
  54.4 4.1 %collective-permute-start.4 = (bf16[4,2,5,32,128]{4,3,2,1,0:T(8,128)(2,1)S(1)}, bf16[4,2,5,32,128]{4,3,2,1,0:T(8,128)(2,1)}, u32[]{:S(2)}, u32[]{:S(2)}) collective-permute-start(bf16[4,2,5,32,128]{4,3,2,1,0:T(8,128)(2,1)S(1)} %collective-permute-done.3.refs_5_), channel_id=1, source_target_pairs={{0,16},{1,17},{2,18},{3,19},{4,20},{5,21},{6,22},{7,23},{24,8},{25... | collective-permute-start | bytes 983048 | tf_op jit(solution)/shard_map/ppermute | solution.py:147
  58.5 1.5 %collective-permute-done.20.refs_6_ = bf16[4,2,5,32,128]{4,3,2,1,0:T(8,128)(2,1)S(1)} collective-permute-done((bf16[4,2,5,32,128]{4,3,2,1,0:T(8,128)(2,1)S(1)}, bf16[4,2,5,32,128]{4,3,2,1,0:T(8,128)(2,1)S(1)}, u32[]{:S(2)}, u32[]{:S(2)}) %collective-permute-start.20) | collective-permute-done | bytes 327712 | tf_op jit(solution)/shard_map/ppermute | solution.py:147
  60.0 0.0 collective-permute-start.23
  60.0 0.1 stack.78
  60.1 0.6 pad_add_fusion.refs_2_
  60.7 6.3 %collective-permute-done.12.refs_6_ = bf16[4,2,5,32,128]{4,3,2,1,0:T(8,128)(2,1)S(1)} collective-permute-done((bf16[4,2,5,32,128]{4,3,2,1,0:T(8,128)(2,1)S(1)}, bf16[4,2,5,32,128]{4,3,2,1,0:T(8,128)(2,1)S(1)}, u32[]{:S(2)}, u32[]{:S(2)}) %collective-permute-start.12) | collective-permute-done | bytes 327712 | tf_op jit(solution)/shard_map/ppermute | solution.py:147
  67.0 0.0 collective-permute-start.14
  67.0 0.0 collective-permute-done.31.refs_9_
  67.0 0.5 collective-permute-start.15
  67.5 7.8 %shard_map.46.refs_10_ = f32[4,384,384]{2,1,0:T(8,128)} custom-call(s32[4]{0:T(128)} %subtract_add_fusion.refs_0_, s32[4,3]{1,0:T(4,128)} %refs_1_.7, s32[2,6]{1,0:T(2,128)} %pad_add_fusion.refs_2_, bf16[4,384,384]{2,1,0:T(8,128)(2,1)} %refs_3_.7, bf16[4,2,5,32,128]{4,3,2,1,0:T(8,128)(2,1)} %copy-done.13, ...), custom_call_target="tpu_custom_call" | custom-call | flops 1811939328 | bytes 6291456 | tf_op jit(solution)/shard_map/pallas_call | solution.py:86
  75.5 0.0 collective-permute-done.22.refs_8_
  75.5 0.1 collective-permute-start.5
  75.6 0.5 collective-permute-start.6
  76.1 0.1 collective-permute-start.7
  76.2 8.7 %shard_map.47.refs_10_ = f32[4,384,384]{2,1,0:T(8,128)} custom-call(s32[4]{0:T(128)} %subtract_add_fusion.refs_0_, s32[4,3]{1,0:T(4,128)} %refs_1_.7, s32[2,6]{1,0:T(2,128)} %pad_add_fusion.refs_2_, bf16[4,384,384]{2,1,0:T(8,128)(2,1)} %refs_3_.7, bf16[4,2,5,32,128]{4,3,2,1,0:T(8,128)(2,1)} %copy-done, bf16[4,2,5,32,128]{4,3,2,1,0:T(8,128)(2,1)} %copy-done.3, ...), custom_call_target="tpu_custom_call" | custom-call | flops 1811939328 | bytes 6291456 | tf_op jit(solution)/shard_map/pallas_call | solution.py:86
  84.9 8.7 %shard_map.48.refs_10_ = f32[4,384,384]{2,1,0:T(8,128)} custom-call(s32[4]{0:T(128)} %subtract_add_fusion.refs_0_, s32[4,3]{1,0:T(4,128)} %refs_1_.7, s32[2,6]{1,0:T(2,128)} %pad_add_fusion.refs_2_, bf16[4,384,384]{2,1,0:T(8,128)(2,1)} %refs_3_.7, bf16[4,2,5,32,128]{4,3,2,1,0:T(8,128)(2,1)} %copy-done.1, bf16[4,2,5,32,128]{4,3,2,1,0:T(8,128)(2,1)} %copy-done.4, ...), custom_call_target="tpu_custom_call" | custom-call | flops 1811939328 | bytes 6291456 | tf_op jit(solution)/shard_map/pallas_call | solution.py:86
  93.6 0.7 copy-done.10
  94.2 0.1 copy-done.11
  94.4 0.7 copy-done.12
  95.1 8.6 %shard_map.49 = f32[4,384,384]{2,1,0:T(8,128)} custom-call(s32[4]{0:T(128)} %subtract_add_fusion.refs_0_, s32[4,3]{1,0:T(4,128)} %refs_1_.7, s32[2,6]{1,0:T(2,128)} %pad_add_fusion.refs_2_, bf16[4,384,384]{2,1,0:T(8,128)(2,1)} %refs_3_.7, bf16[4,2,5,32,128]{4,3,2,1,0:T(8,128)(2,1)} %copy-done.2, bf16[4,2,5,32,128]{4,3,2,1,0:T(8,128)(2,1)} %copy-done.7, ...), custom_call_target="tpu_custom_call" | custom-call | flops 1811939328 | bytes 6291456 | tf_op jit(solution)/shard_map/pallas_call | solution.py:86
  (45 shorter events, 0.3 us)
Async XLA Ops:
  0.0 53.3 %copy-start.15 = (s32[4]{0:T(128)S(1)}, s32[4]{0:T(128)}, u32[]{:S(2)}) copy-start(s32[4]{0:T(128)} %param.6) | copy-start | bytes 52
  1.1 10.1 %collective-permute-start.24 = (bf16[2,5,32,128]{3,2,1,0:T(8,128)(2,1)S(1)}, bf16[2,5,32,128]{3,2,1,0:T(8,128)(2,1)S(1)}, u32[]{:S(2)}, u32[]{:S(2)}) collective-permute-start(bf16[2,5,32,128]{3,2,1,0:T(8,128)(2,1)S(1)} %get-tuple-element.9), channel_id=1, source_target_pairs={{0,1},{1,0},{2,3},{3,2},{4,5},{5,4},{6,7},{7,6},{8,9},{9,8},{10,11... | collective-permute-start | bytes 245768 | tf_op jit(solution)/shard_map/ppermute | solution.py:145
  4.2 10.3 %collective-permute-start.25 = (bf16[2,5,32,128]{3,2,1,0:T(8,128)(2,1)S(1)}, bf16[2,5,32,128]{3,2,1,0:T(8,128)(2,1)S(1)}, u32[]{:S(2)}, u32[]{:S(2)}) collective-permute-start(bf16[2,5,32,128]{3,2,1,0:T(8,128)(2,1)S(1)} %get-tuple-element.9), channel_id=1, source_target_pairs={{0,2},{1,3},{2,0},{3,1},{4,6},{5,7},{6,4},{7,5},{8,10},{9,11},{10,... | collective-permute-start | bytes 245768 | tf_op jit(solution)/shard_map/ppermute | solution.py:145
  6.8 7.7 %collective-permute-start.26 = (bf16[2,5,32,128]{3,2,1,0:T(8,128)(2,1)S(1)}, bf16[2,5,32,128]{3,2,1,0:T(8,128)(2,1)S(1)}, u32[]{:S(2)}, u32[]{:S(2)}) collective-permute-start(bf16[2,5,32,128]{3,2,1,0:T(8,128)(2,1)S(1)} %get-tuple-element.9), channel_id=1, source_target_pairs={{0,3},{1,2},{2,1},{3,0},{4,7},{5,6},{6,5},{7,4},{8,11},{9,10},{10,... | collective-permute-start | bytes 245768 | tf_op jit(solution)/shard_map/ppermute | solution.py:145
  6.8 15.5 %collective-permute-start.16 = (bf16[2,5,32,128]{3,2,1,0:T(8,128)(2,1)S(1)}, bf16[2,5,32,128]{3,2,1,0:T(8,128)(2,1)S(1)}, u32[]{:S(2)}, u32[]{:S(2)}) collective-permute-start(bf16[2,5,32,128]{3,2,1,0:T(8,128)(2,1)S(1)} %get-tuple-element.8), channel_id=1, source_target_pairs={{0,1},{1,0},{2,3},{3,2},{4,5},{5,4},{6,7},{7,6},{8,9},{9,8},{10,11... | collective-permute-start | bytes 245768 | tf_op jit(solution)/shard_map/ppermute | solution.py:145
  7.7 15.0 %collective-permute-start.17 = (bf16[2,5,32,128]{3,2,1,0:T(8,128)(2,1)S(1)}, bf16[2,5,32,128]{3,2,1,0:T(8,128)(2,1)S(1)}, u32[]{:S(2)}, u32[]{:S(2)}) collective-permute-start(bf16[2,5,32,128]{3,2,1,0:T(8,128)(2,1)S(1)} %get-tuple-element.8), channel_id=1, source_target_pairs={{0,2},{1,3},{2,0},{3,1},{4,6},{5,7},{6,4},{7,5},{8,10},{9,11},{10,... | collective-permute-start | bytes 245768 | tf_op jit(solution)/shard_map/ppermute | solution.py:145
  11.2 13.0 %collective-permute-start.18 = (bf16[2,5,32,128]{3,2,1,0:T(8,128)(2,1)S(1)}, bf16[2,5,32,128]{3,2,1,0:T(8,128)(2,1)S(1)}, u32[]{:S(2)}, u32[]{:S(2)}) collective-permute-start(bf16[2,5,32,128]{3,2,1,0:T(8,128)(2,1)S(1)} %get-tuple-element.8), channel_id=1, source_target_pairs={{0,3},{1,2},{2,1},{3,0},{4,7},{5,6},{6,5},{7,4},{8,11},{9,10},{10,... | collective-permute-start | bytes 245768 | tf_op jit(solution)/shard_map/ppermute | solution.py:145
  14.5 9.8 %collective-permute-start.8 = (bf16[2,5,32,128]{3,2,1,0:T(8,128)(2,1)S(1)}, bf16[2,5,32,128]{3,2,1,0:T(8,128)(2,1)S(1)}, u32[]{:S(2)}, u32[]{:S(2)}) collective-permute-start(bf16[2,5,32,128]{3,2,1,0:T(8,128)(2,1)S(1)} %get-tuple-element.7), channel_id=1, source_target_pairs={{0,1},{1,0},{2,3},{3,2},{4,5},{5,4},{6,7},{7,6},{8,9},{9,8},{10,11... | collective-permute-start | bytes 245768 | tf_op jit(solution)/shard_map/ppermute | solution.py:145
  14.5 12.1 %collective-permute-start.9 = (bf16[2,5,32,128]{3,2,1,0:T(8,128)(2,1)S(1)}, bf16[2,5,32,128]{3,2,1,0:T(8,128)(2,1)S(1)}, u32[]{:S(2)}, u32[]{:S(2)}) collective-permute-start(bf16[2,5,32,128]{3,2,1,0:T(8,128)(2,1)S(1)} %get-tuple-element.7), channel_id=1, source_target_pairs={{0,2},{1,3},{2,0},{3,1},{4,6},{5,7},{6,4},{7,5},{8,10},{9,11},{10,... | collective-permute-start | bytes 245768 | tf_op jit(solution)/shard_map/ppermute | solution.py:145
  22.3 18.6 %copy-start.13 = (bf16[4,2,5,32,128]{4,3,2,1,0:T(8,128)(2,1)}, bf16[4,2,5,32,128]{4,3,2,1,0:T(8,128)(2,1)S(1)}, u32[]{:S(2)}) copy-start(bf16[4,2,5,32,128]{4,3,2,1,0:T(8,128)(2,1)S(1)} %pad_maximum_fusion.3.refs_4_) | copy-start | bytes 983044
  22.3 6.4 %collective-permute-start.10 = (bf16[2,5,32,128]{3,2,1,0:T(8,128)(2,1)S(1)}, bf16[2,5,32,128]{3,2,1,0:T(8,128)(2,1)S(1)}, u32[]{:S(2)}, u32[]{:S(2)}) collective-permute-start(bf16[2,5,32,128]{3,2,1,0:T(8,128)(2,1)S(1)} %get-tuple-element.7), channel_id=1, source_target_pairs={{0,3},{1,2},{2,1},{3,0},{4,7},{5,6},{6,5},{7,4},{8,11},{9,10},{10,... | collective-permute-start | bytes 245768 | tf_op jit(solution)/shard_map/ppermute | solution.py:145
  22.7 14.1 %collective-permute-start.27 = (bf16[4,2,5,32,128]{4,3,2,1,0:T(8,128)(2,1)S(1)}, bf16[4,2,5,32,128]{4,3,2,1,0:T(8,128)(2,1)}, u32[]{:S(2)}, u32[]{:S(2)}) collective-permute-start(bf16[4,2,5,32,128]{4,3,2,1,0:T(8,128)(2,1)S(1)} %pad_maximum_fusion.3.refs_4_), channel_id=1, source_target_pairs={{0,8},{1,9},{2,10},{3,11},{4,12},{5,13},{6,14},{7,15},{8,0},{9,1},... | collective-permute-start | bytes 983048 | tf_op jit(solution)/shard_map/ppermute | solution.py:146
  24.2 12.6 %collective-permute-start.29 = (bf16[4,2,5,32,128]{4,3,2,1,0:T(8,128)(2,1)S(1)}, bf16[4,2,5,32,128]{4,3,2,1,0:T(8,128)(2,1)S(1)}, u32[]{:S(2)}, u32[]{:S(2)}) collective-permute-start(bf16[4,2,5,32,128]{4,3,2,1,0:T(8,128)(2,1)S(1)} %pad_maximum_fusion.3.refs_4_), channel_id=1, source_target_pairs={{0,4},{1,5},{2,6},{3,7},{4,0},{5,1},{6,2},{7,3},{8,12},{9,13},{10,... | collective-permute-start | bytes 983048 | tf_op jit(solution)/shard_map/ppermute | solution.py:149
  24.2 51.1 %copy-start = (bf16[4,2,5,32,128]{4,3,2,1,0:T(8,128)(2,1)}, bf16[4,2,5,32,128]{4,3,2,1,0:T(8,128)(2,1)S(1)}, u32[]{:S(2)}) copy-start(bf16[4,2,5,32,128]{4,3,2,1,0:T(8,128)(2,1)S(1)} %pad_maximum_fusion.2.refs_4_) | copy-start | bytes 983044
  24.3 6.7 %collective-permute-start = (bf16[2,5,32,128]{3,2,1,0:T(8,128)(2,1)S(1)}, bf16[2,5,32,128]{3,2,1,0:T(8,128)(2,1)S(1)}, u32[]{:S(2)}, u32[]{:S(2)}) collective-permute-start(bf16[2,5,32,128]{3,2,1,0:T(8,128)(2,1)S(1)} %get-tuple-element.6), channel_id=1, source_target_pairs={{0,1},{1,0},{2,3},{3,2},{4,5},{5,4},{6,7},{7,6},{8,9},{9,8},{10,11... | collective-permute-start | bytes 245768 | tf_op jit(solution)/shard_map/ppermute | solution.py:145
  26.6 9.5 %collective-permute-start.1 = (bf16[2,5,32,128]{3,2,1,0:T(8,128)(2,1)S(1)}, bf16[2,5,32,128]{3,2,1,0:T(8,128)(2,1)S(1)}, u32[]{:S(2)}, u32[]{:S(2)}) collective-permute-start(bf16[2,5,32,128]{3,2,1,0:T(8,128)(2,1)S(1)} %get-tuple-element.6), channel_id=1, source_target_pairs={{0,2},{1,3},{2,0},{3,1},{4,6},{5,7},{6,4},{7,5},{8,10},{9,11},{10,... | collective-permute-start | bytes 245768 | tf_op jit(solution)/shard_map/ppermute | solution.py:145
  28.8 7.3 %collective-permute-start.2 = (bf16[2,5,32,128]{3,2,1,0:T(8,128)(2,1)S(1)}, bf16[2,5,32,128]{3,2,1,0:T(8,128)(2,1)S(1)}, u32[]{:S(2)}, u32[]{:S(2)}) collective-permute-start(bf16[2,5,32,128]{3,2,1,0:T(8,128)(2,1)S(1)} %get-tuple-element.6), channel_id=1, source_target_pairs={{0,3},{1,2},{2,1},{3,0},{4,7},{5,6},{6,5},{7,4},{8,11},{9,10},{10,... | collective-permute-start | bytes 245768 | tf_op jit(solution)/shard_map/ppermute | solution.py:145
  30.0 45.4 %copy-start.1 = (bf16[4,2,5,32,128]{4,3,2,1,0:T(8,128)(2,1)}, bf16[4,2,5,32,128]{4,3,2,1,0:T(8,128)(2,1)S(1)}, u32[]{:S(2)}) copy-start(bf16[4,2,5,32,128]{4,3,2,1,0:T(8,128)(2,1)S(1)} %pad_maximum_fusion.1.refs_4_) | copy-start | bytes 983044
  30.9 10.4 %collective-permute-start.19 = (bf16[4,2,5,32,128]{4,3,2,1,0:T(8,128)(2,1)S(1)}, bf16[4,2,5,32,128]{4,3,2,1,0:T(8,128)(2,1)S(1)}, u32[]{:S(2)}, u32[]{:S(2)}) collective-permute-start(bf16[4,2,5,32,128]{4,3,2,1,0:T(8,128)(2,1)S(1)} %pad_maximum_fusion.2.refs_4_), channel_id=1, source_target_pairs={{0,8},{1,9},{2,10},{3,11},{4,12},{5,13},{6,14},{7,15},{8,0},{9,1},... | collective-permute-start | bytes 983048 | tf_op jit(solution)/shard_map/ppermute | solution.py:146
  36.1 6.1 %collective-permute-start.21 = (bf16[4,2,5,32,128]{4,3,2,1,0:T(8,128)(2,1)S(1)}, bf16[4,2,5,32,128]{4,3,2,1,0:T(8,128)(2,1)S(1)}, u32[]{:S(2)}, u32[]{:S(2)}) collective-permute-start(bf16[4,2,5,32,128]{4,3,2,1,0:T(8,128)(2,1)S(1)} %pad_maximum_fusion.2.refs_4_), channel_id=1, source_target_pairs={{0,4},{1,5},{2,6},{3,7},{4,0},{5,1},{6,2},{7,3},{8,12},{9,13},{10,... | collective-permute-start | bytes 983048 | tf_op jit(solution)/shard_map/ppermute | solution.py:149
  36.1 12.4 %collective-permute-start.11 = (bf16[4,2,5,32,128]{4,3,2,1,0:T(8,128)(2,1)S(1)}, bf16[4,2,5,32,128]{4,3,2,1,0:T(8,128)(2,1)S(1)}, u32[]{:S(2)}, u32[]{:S(2)}) collective-permute-start(bf16[4,2,5,32,128]{4,3,2,1,0:T(8,128)(2,1)S(1)} %pad_maximum_fusion.1.refs_4_), channel_id=1, source_target_pairs={{0,8},{1,9},{2,10},{3,11},{4,12},{5,13},{6,14},{7,15},{8,0},{9,1},... | collective-permute-start | bytes 983048 | tf_op jit(solution)/shard_map/ppermute | solution.py:146
  36.8 15.1 %collective-permute-start.13 = (bf16[4,2,5,32,128]{4,3,2,1,0:T(8,128)(2,1)S(1)}, bf16[4,2,5,32,128]{4,3,2,1,0:T(8,128)(2,1)S(1)}, u32[]{:S(2)}, u32[]{:S(2)}) collective-permute-start(bf16[4,2,5,32,128]{4,3,2,1,0:T(8,128)(2,1)S(1)} %pad_maximum_fusion.1.refs_4_), channel_id=1, source_target_pairs={{0,4},{1,5},{2,6},{3,7},{4,0},{5,1},{6,2},{7,3},{8,12},{9,13},{10,... | collective-permute-start | bytes 983048 | tf_op jit(solution)/shard_map/ppermute | solution.py:149
  36.8 11.6 %copy-start.14 = (bf16[4,2,5,32,128]{4,3,2,1,0:T(8,128)(2,1)}, bf16[4,2,5,32,128]{4,3,2,1,0:T(8,128)(2,1)S(1)}, u32[]{:S(2)}) copy-start(bf16[4,2,5,32,128]{4,3,2,1,0:T(8,128)(2,1)S(1)} %collective-permute-done.29.refs_7_) | copy-start | bytes 983044
  36.8 16.4 %collective-permute-start.28 = (bf16[4,2,5,32,128]{4,3,2,1,0:T(8,128)(2,1)}, bf16[4,2,5,32,128]{4,3,2,1,0:T(8,128)(2,1)}, u32[]{:S(2)}, u32[]{:S(2)}) collective-permute-start(bf16[4,2,5,32,128]{4,3,2,1,0:T(8,128)(2,1)} %collective-permute-done.27.refs_5_), channel_id=1, source_target_pairs={{0,16},{1,17},{2,18},{3,19},{4,20},{5,21},{6,22},{7,23},{24,8},{25... | collective-permute-start | bytes 983048 | tf_op jit(solution)/shard_map/ppermute | solution.py:147
  41.0 34.5 %copy-start.2 = (bf16[4,2,5,32,128]{4,3,2,1,0:T(8,128)(2,1)}, bf16[4,2,5,32,128]{4,3,2,1,0:T(8,128)(2,1)S(1)}, u32[]{:S(2)}) copy-start(bf16[4,2,5,32,128]{4,3,2,1,0:T(8,128)(2,1)S(1)} %pad_maximum_fusion.refs_4_) | copy-start | bytes 983044
  41.4 34.0 %copy-start.3 = (bf16[4,2,5,32,128]{4,3,2,1,0:T(8,128)(2,1)}, bf16[4,2,5,32,128]{4,3,2,1,0:T(8,128)(2,1)S(1)}, u32[]{:S(2)}) copy-start(bf16[4,2,5,32,128]{4,3,2,1,0:T(8,128)(2,1)S(1)} %collective-permute-done.19.refs_5_) | copy-start | bytes 983044
  41.4 13.0 %collective-permute-start.3 = (bf16[4,2,5,32,128]{4,3,2,1,0:T(8,128)(2,1)S(1)}, bf16[4,2,5,32,128]{4,3,2,1,0:T(8,128)(2,1)S(1)}, u32[]{:S(2)}, u32[]{:S(2)}) collective-permute-start(bf16[4,2,5,32,128]{4,3,2,1,0:T(8,128)(2,1)S(1)} %pad_maximum_fusion.refs_4_), channel_id=1, source_target_pairs={{0,8},{1,9},{2,10},{3,11},{4,12},{5,13},{6,14},{7,15},{8,0},{9,1},... | collective-permute-start | bytes 983048 | tf_op jit(solution)/shard_map/ppermute | solution.py:146
  42.2 33.3 %copy-start.5 = (bf16[4,2,5,32,128]{4,3,2,1,0:T(8,128)(2,1)}, bf16[4,2,5,32,128]{4,3,2,1,0:T(8,128)(2,1)S(1)}, u32[]{:S(2)}) copy-start(bf16[4,2,5,32,128]{4,3,2,1,0:T(8,128)(2,1)S(1)} %collective-permute-done.21.refs_7_) | copy-start | bytes 983044
  42.2 12.2 %collective-permute-start.30 = (bf16[4,2,5,32,128]{4,3,2,1,0:T(8,128)(2,1)}, bf16[4,2,5,32,128]{4,3,2,1,0:T(8,128)(2,1)}, u32[]{:S(2)}, u32[]{:S(2)}) collective-permute-start(bf16[4,2,5,32,128]{4,3,2,1,0:T(8,128)(2,1)} %collective-permute-done.27.refs_5_), channel_id=1, source_target_pairs={{0,4},{1,5},{2,6},{3,7},{4,0},{5,1},{6,2},{7,3},{8,12},{9,13},{10,... | collective-permute-start | bytes 983048 | tf_op jit(solution)/shard_map/ppermute | solution.py:149
  48.4 27.0 %copy-start.4 = (bf16[4,2,5,32,128]{4,3,2,1,0:T(8,128)(2,1)}, bf16[4,2,5,32,128]{4,3,2,1,0:T(8,128)(2,1)S(1)}, u32[]{:S(2)}) copy-start(bf16[4,2,5,32,128]{4,3,2,1,0:T(8,128)(2,1)S(1)} %collective-permute-done.11.refs_5_) | copy-start | bytes 983044
  48.4 11.6 %collective-permute-start.20 = (bf16[4,2,5,32,128]{4,3,2,1,0:T(8,128)(2,1)S(1)}, bf16[4,2,5,32,128]{4,3,2,1,0:T(8,128)(2,1)S(1)}, u32[]{:S(2)}, u32[]{:S(2)}) collective-permute-start(bf16[4,2,5,32,128]{4,3,2,1,0:T(8,128)(2,1)S(1)} %collective-permute-done.19.refs_5_), channel_id=1, source_target_pairs={{0,16},{1,17},{2,18},{3,19},{4,20},{5,21},{6,22},{7,23},{24,8},{25... | collective-permute-start | bytes 983048 | tf_op jit(solution)/shard_map/ppermute | solution.py:147
  51.9 23.6 %copy-start.6 = (bf16[4,2,5,32,128]{4,3,2,1,0:T(8,128)(2,1)}, bf16[4,2,5,32,128]{4,3,2,1,0:T(8,128)(2,1)S(1)}, u32[]{:S(2)}) copy-start(bf16[4,2,5,32,128]{4,3,2,1,0:T(8,128)(2,1)S(1)} %collective-permute-done.13.refs_7_) | copy-start | bytes 983044
  51.9 15.1 %collective-permute-start.12 = (bf16[4,2,5,32,128]{4,3,2,1,0:T(8,128)(2,1)S(1)}, bf16[4,2,5,32,128]{4,3,2,1,0:T(8,128)(2,1)S(1)}, u32[]{:S(2)}, u32[]{:S(2)}) collective-permute-start(bf16[4,2,5,32,128]{4,3,2,1,0:T(8,128)(2,1)S(1)} %collective-permute-done.11.refs_5_), channel_id=1, source_target_pairs={{0,16},{1,17},{2,18},{3,19},{4,20},{5,21},{6,22},{7,23},{24,8},{25... | collective-permute-start | bytes 983048 | tf_op jit(solution)/shard_map/ppermute | solution.py:147
  53.2 13.8 %collective-permute-start.31 = (bf16[4,2,5,32,128]{4,3,2,1,0:T(8,128)(2,1)}, bf16[4,2,5,32,128]{4,3,2,1,0:T(8,128)(2,1)}, u32[]{:S(2)}, u32[]{:S(2)}) collective-permute-start(bf16[4,2,5,32,128]{4,3,2,1,0:T(8,128)(2,1)} %collective-permute-done.28.refs_6_), channel_id=1, source_target_pairs={{0,4},{1,5},{2,6},{3,7},{4,0},{5,1},{6,2},{7,3},{8,12},{9,13},{10,... | collective-permute-start | bytes 983048 | tf_op jit(solution)/shard_map/ppermute | solution.py:149
  54.4 21.3 %copy-start.7 = (bf16[4,2,5,32,128]{4,3,2,1,0:T(8,128)(2,1)}, bf16[4,2,5,32,128]{4,3,2,1,0:T(8,128)(2,1)S(1)}, u32[]{:S(2)}) copy-start(bf16[4,2,5,32,128]{4,3,2,1,0:T(8,128)(2,1)S(1)} %collective-permute-done.3.refs_5_) | copy-start | bytes 983044
  54.4 21.1 %collective-permute-start.22 = (bf16[4,2,5,32,128]{4,3,2,1,0:T(8,128)(2,1)S(1)}, bf16[4,2,5,32,128]{4,3,2,1,0:T(8,128)(2,1)}, u32[]{:S(2)}, u32[]{:S(2)}) collective-permute-start(bf16[4,2,5,32,128]{4,3,2,1,0:T(8,128)(2,1)S(1)} %collective-permute-done.19.refs_5_), channel_id=1, source_target_pairs={{0,4},{1,5},{2,6},{3,7},{4,0},{5,1},{6,2},{7,3},{8,12},{9,13},{10,... | collective-permute-start | bytes 983048 | tf_op jit(solution)/shard_map/ppermute | solution.py:149
  54.4 21.2 %collective-permute-start.4 = (bf16[4,2,5,32,128]{4,3,2,1,0:T(8,128)(2,1)S(1)}, bf16[4,2,5,32,128]{4,3,2,1,0:T(8,128)(2,1)}, u32[]{:S(2)}, u32[]{:S(2)}) collective-permute-start(bf16[4,2,5,32,128]{4,3,2,1,0:T(8,128)(2,1)S(1)} %collective-permute-done.3.refs_5_), channel_id=1, source_target_pairs={{0,16},{1,17},{2,18},{3,19},{4,20},{5,21},{6,22},{7,23},{24,8},{25... | collective-permute-start | bytes 983048 | tf_op jit(solution)/shard_map/ppermute | solution.py:147
  60.0 15.5 %copy-start.8 = (bf16[4,2,5,32,128]{4,3,2,1,0:T(8,128)(2,1)}, bf16[4,2,5,32,128]{4,3,2,1,0:T(8,128)(2,1)S(1)}, u32[]{:S(2)}) copy-start(bf16[4,2,5,32,128]{4,3,2,1,0:T(8,128)(2,1)S(1)} %collective-permute-done.20.refs_6_) | copy-start | bytes 983044
  60.0 16.1 %collective-permute-start.23 = (bf16[4,2,5,32,128]{4,3,2,1,0:T(8,128)(2,1)S(1)}, bf16[4,2,5,32,128]{4,3,2,1,0:T(8,128)(2,1)}, u32[]{:S(2)}, u32[]{:S(2)}) collective-permute-start(bf16[4,2,5,32,128]{4,3,2,1,0:T(8,128)(2,1)S(1)} %collective-permute-done.20.refs_6_), channel_id=1, source_target_pairs={{0,4},{1,5},{2,6},{3,7},{4,0},{5,1},{6,2},{7,3},{8,12},{9,13},{10,... | collective-permute-start | bytes 983048 | tf_op jit(solution)/shard_map/ppermute | solution.py:149
  67.0 8.4 %copy-start.9 = (bf16[4,2,5,32,128]{4,3,2,1,0:T(8,128)(2,1)}, bf16[4,2,5,32,128]{4,3,2,1,0:T(8,128)(2,1)S(1)}, u32[]{:S(2)}) copy-start(bf16[4,2,5,32,128]{4,3,2,1,0:T(8,128)(2,1)S(1)} %collective-permute-done.12.refs_6_) | copy-start | bytes 983044
  67.0 17.8 %collective-permute-start.14 = (bf16[4,2,5,32,128]{4,3,2,1,0:T(8,128)(2,1)S(1)}, bf16[4,2,5,32,128]{4,3,2,1,0:T(8,128)(2,1)}, u32[]{:S(2)}, u32[]{:S(2)}) collective-permute-start(bf16[4,2,5,32,128]{4,3,2,1,0:T(8,128)(2,1)S(1)} %collective-permute-done.11.refs_5_), channel_id=1, source_target_pairs={{0,4},{1,5},{2,6},{3,7},{4,0},{5,1},{6,2},{7,3},{8,12},{9,13},{10,... | collective-permute-start | bytes 983048 | tf_op jit(solution)/shard_map/ppermute | solution.py:149
  67.0 17.8 %collective-permute-start.15 = (bf16[4,2,5,32,128]{4,3,2,1,0:T(8,128)(2,1)S(1)}, bf16[4,2,5,32,128]{4,3,2,1,0:T(8,128)(2,1)}, u32[]{:S(2)}, u32[]{:S(2)}) collective-permute-start(bf16[4,2,5,32,128]{4,3,2,1,0:T(8,128)(2,1)S(1)} %collective-permute-done.12.refs_6_), channel_id=1, source_target_pairs={{0,4},{1,5},{2,6},{3,7},{4,0},{5,1},{6,2},{7,3},{8,12},{9,13},{10,... | collective-permute-start | bytes 983048 | tf_op jit(solution)/shard_map/ppermute | solution.py:149
  75.5 18.0 %collective-permute-start.5 = (bf16[4,2,5,32,128]{4,3,2,1,0:T(8,128)(2,1)S(1)}, bf16[4,2,5,32,128]{4,3,2,1,0:T(8,128)(2,1)S(1)}, u32[]{:S(2)}, u32[]{:S(2)}) collective-permute-start(bf16[4,2,5,32,128]{4,3,2,1,0:T(8,128)(2,1)S(1)} %pad_maximum_fusion.refs_4_), channel_id=1, source_target_pairs={{0,4},{1,5},{2,6},{3,7},{4,0},{5,1},{6,2},{7,3},{8,12},{9,13},{10,... | collective-permute-start | bytes 983048 | tf_op jit(solution)/shard_map/ppermute | solution.py:149
  75.6 17.9 %collective-permute-start.6 = (bf16[4,2,5,32,128]{4,3,2,1,0:T(8,128)(2,1)S(1)}, bf16[4,2,5,32,128]{4,3,2,1,0:T(8,128)(2,1)S(1)}, u32[]{:S(2)}, u32[]{:S(2)}) collective-permute-start(bf16[4,2,5,32,128]{4,3,2,1,0:T(8,128)(2,1)S(1)} %collective-permute-done.3.refs_5_), channel_id=1, source_target_pairs={{0,4},{1,5},{2,6},{3,7},{4,0},{5,1},{6,2},{7,3},{8,12},{9,13},{10,... | collective-permute-start | bytes 983048 | tf_op jit(solution)/shard_map/ppermute | solution.py:149
  76.1 17.5 %collective-permute-start.7 = (bf16[4,2,5,32,128]{4,3,2,1,0:T(8,128)(2,1)}, bf16[4,2,5,32,128]{4,3,2,1,0:T(8,128)(2,1)S(1)}, u32[]{:S(2)}, u32[]{:S(2)}) collective-permute-start(bf16[4,2,5,32,128]{4,3,2,1,0:T(8,128)(2,1)} %collective-permute-done.4.refs_6_), channel_id=1, source_target_pairs={{0,4},{1,5},{2,6},{3,7},{4,0},{5,1},{6,2},{7,3},{8,12},{9,13},{10,... | collective-permute-start | bytes 983048 | tf_op jit(solution)/shard_map/ppermute | solution.py:149
  93.5 0.7 copy-start.10
  93.5 0.8 copy-start.11
  94.4 0.7 copy-start.12

commit v2 on v0

v2 whole, which is shorter than its diff:
```python
import functools

import jax
import jax.numpy as jnp
from jax import lax
from jax.experimental import pallas as pl
from jax.experimental.pallas import tpu as pltpu
from jax.sharding import PartitionSpec as P

VB = 128
DW = 3
PANELS = 6
CHUNKS = (1, 1, 1, 1)
KGROUPS = ((0,), (1,), (2,), (3,))
OWN_FIRST = True
DEPS = {'x_3': ['k_0'], 'y_3': ['k_1'], 'z_2': ['x_own']}
AXES = ("vblk", "pair")


def ladder_kernel(plan, chunk, sets, npanel, has_sum, *refs):
    refs = list(refs)
    place_ref = refs.pop(0)
    info_refs = [refs.pop(0) for _ in range(sets)]
    amp_refs = [refs.pop(0) for _ in range(sets)]
    panel_refs = [refs.pop(0) for _ in range(npanel)]
    sum_refs = [refs.pop(0) for _ in range(sets)] if has_sum else []
    out_refs = [refs.pop(0) for _ in range(sets)]
    tiles, strips, halves, sem = refs
    core = place_ref[0]

    copies = []
    for i, group, slot, row0, source, first, size in plan:
        shard = panel_refs[i]
        rows = shard.shape[-2]
        row = pl.multiple_of(place_ref[4 + row0] * rows, rows)
        at = pl.multiple_of(2 * place_ref[1 + group], 2)
        view = shard.at[:, pl.ds(source, size)] if slot is None else shard.at[slot, :, pl.ds(source, size)]
        copies.append(
            pltpu.make_async_copy(
                view, tiles.at[pl.ds(at, 2), pl.ds(first, size), :, pl.ds(row, rows), :], sem.at[len(copies)]
            )
        )
    for copy in copies:
        copy.start()
    for copy in copies:
        copy.wait()

    for k in range(sets):
        info_ref, amp_ref, out_ref = info_refs[k], amp_refs[k], out_refs[k]

        @pl.loop(0, amp_ref.shape[0])
        def _(p):
            rel = info_ref[p, 0]
            live = [info_ref[p, 1 + a] > 0 for a in range(DW)]
            masked = jnp.concatenate(
                [
                    jnp.concatenate(
                        [
                            jnp.where(live[a] & live[b], amp_ref[p, pl.ds(a * VB, VB), pl.ds(b * VB, VB)], 0)
                            for b in range(DW)
                        ],
                        axis=1,
                    )
                    for a in range(DW)
                ],
                axis=0,
            ).astype(jnp.bfloat16)
            for j in range(chunk):
                for a in range(DW):
                    d = jnp.bitwise_xor(rel + a, core)
                    strips[pl.ds(a * VB, VB), pl.ds(j * DW * VB, DW * VB)] = jnp.concatenate(
                        [tiles[d, j, b - a + DW - 1] for b in range(DW)], axis=1
                    )
            for j in range(chunk):
                cols = pl.ds(j * DW * VB, DW * VB)
                halves[:, cols] = jnp.dot(
                    strips[:, cols], masked, preferred_element_type=jnp.float32
                ).astype(jnp.bfloat16)
            ladder = lax.dot_general(
                halves[...], strips[...], (((1,), (1,)), ((), ())), preferred_element_type=jnp.float32
            )
            for a in range(DW):
                for b in range(DW):
                    at = (p, pl.ds(a * VB, VB), pl.ds(b * VB, VB))
                    part = ladder[a * VB : (a + 1) * VB, b * VB : (b + 1) * VB]
                    if has_sum:
                        part = part + sum_refs[k][at]
                    out_ref[at] = jnp.where(live[a] & live[b], part, 0.0)


def ladder(plan, chunk, place, pairs, panels, totals):
    infos, amps = zip(*pairs)
    npair, width, _ = amps[0].shape
    sets = len(pairs)
    vmem = pl.BlockSpec(memory_space=pltpu.VMEM)
    smem = pl.BlockSpec(memory_space=pltpu.SMEM)
    offs, rows, vb = panels[0].shape[-3:]
    totals = totals or []
    at = 1 + 2 * sets + len(panels)
    return pl.pallas_call(
        functools.partial(ladder_kernel, plan, chunk, sets, len(panels), bool(totals)),
        out_shape=[jax.ShapeDtypeStruct((npair, width, width), jnp.float32)] * sets,
        in_specs=[smem] * (1 + sets) + [vmem] * (sets + len(panels) + len(totals)),
        out_specs=[vmem] * sets,
        scratch_shapes=[
            pltpu.VMEM((PANELS, chunk, offs, VB, vb), jnp.bfloat16),
            pltpu.VMEM((width, chunk * width), jnp.bfloat16),
            pltpu.VMEM((width, chunk * width), jnp.bfloat16),
            pltpu.SemaphoreType.DMA((len(plan),)),
        ],
        input_output_aliases={at + k: k for k in range(len(totals))},
        compiler_params=pltpu.CompilerParams(vmem_limit_bytes=24 << 20),
        cost_estimate=pl.CostEstimate(
            flops=sets * npair * chunk * 4 * width**3, bytes_accessed=8 << 20, transcendentals=0
        ),
    )(place, *infos, *amps, *panels, *totals)


def after(x, *tokens):
    return lax.optimization_barrier((x, *tokens))[0]


def solution(mesh):
    nv, nz = mesh.shape["vblk"], mesh.shape["pair"]
    chips = nv // 2

    def moves(step):
        pairs = []
        for v in range(nv):
            for z in range(nz):
                to = step(v // 2, v % 2, z)
                if to is not None and 0 <= to[0] < chips:
                    pairs.append((v * nz + z, (to[0] * 2 + to[1]) * nz + to[2]))
        return pairs

    sideways = [moves(lambda i, c, z, s=s: (i, c, z ^ s)) for s in range(1, nz)]
    neighbour = moves(lambda i, c, z: (i ^ 1, c, z))
    relay = moves(lambda i, c, z: (i - 2 if i % 2 else i + 2, c, z))
    sibling = moves(lambda i, c, z: (i, 1 - c, z))

    def send(x, pairs, name):
        with jax.named_scope(name):
            return lax.ppermute(x, AXES, pairs)

    def local(amplitudes, domain_mask, centers, chol_panel):
        v = lax.axis_index("vblk")
        z = lax.axis_index("pair")
        core = v & 1
        odd = (v >> 1) & 1
        near = 2 - 2 * odd
        place = jnp.where(
            jnp.arange(8) < 4,
            jnp.where(
                jnp.arange(8) == 0,
                core,
                jnp.where(jnp.arange(8) == 1, 1, jnp.where(jnp.arange(8) == 2, near, 2 - near)),
            ),
            z ^ (jnp.arange(8) - 4),
        ).astype(jnp.int32)
        half = chol_panel.shape[1] // 2
        mine = lax.dynamic_slice_in_dim(chol_panel[0], core * half, half, axis=0)
        give = lax.dynamic_slice_in_dim(chol_panel[0], (1 - core) * half, half, axis=0)
        own = jnp.stack([mine, send(give, sibling, "give")])
        rel = centers - (v - core) + 1
        info = jnp.concatenate([rel[:, None], domain_mask], axis=1)
        memo = {}
        starts = [sum(CHUNKS[:j]) for j in range(len(CHUNKS))]
        first_slot = 1 if OWN_FIRST else 0

        def operand(kind, j):
            if kind == "z":
                return own[:, starts[j] : starts[j] + CHUNKS[j]]
            if kind == "x":
                return own if j == "own" else get("g", j)
            if kind == "y":
                return get("x", j)
            return {"far": amplitudes, "info": info}[j]

        def get(kind, j):
            name = f"{kind}_{j}"
            if name not in memo:
                if kind == "g":
                    part = operand("z", j)
                    memo[name] = jnp.stack(([] if OWN_FIRST else [part]) + get("z", j))
                elif kind == "k":
                    memo[name] = run(j)
                else:
                    x = operand(kind, j)
                    tokens = [t for d in DEPS.get(name, ()) for t in jax.tree.leaves(get(*spelt(d)))]
                    if tokens:
                        x = after(x, *tokens)
                    if kind == "z":
                        memo[name] = [send(x, m, name) for m in sideways]
                    else:
                        memo[name] = send(x, {"x": neighbour, "y": relay, "p": sibling}[kind], name)
            return memo[name]

        def spelt(d):
            kind, j = d.split("_")
            return kind, int(j) if j.isdigit() else j

        def run(g):
            group = KGROUPS[g]
            panels, plan, first = [], [], 0
            for j in group:
                if OWN_FIRST:
                    if j == group[0]:
                        panels += [own, get("x", "own"), get("y", "own")]
                    for i in range(3):
                        plan.append((i, i, None, 0, starts[j], first, CHUNKS[j]))
                got = [get("g", j), get("x", j), get("y", j)]
                for i in range(3):
                    for s in range(nz - first_slot):
                        plan.append((len(panels) + i, i, s, s + first_slot, 0, first, CHUNKS[j]))
                panels += got
                first += CHUNKS[j]
            pairs = [(info, amplitudes), (get("p", "info"), get("p", "far"))]
            totals = get("k", g - 1) if g else None
            if g < len(KGROUPS) - 1:
                return ladder(plan, first, place, pairs, panels, totals)
            theirs = ladder(plan, first, place, pairs[1:], panels, totals and totals[1:])
            ours = ladder(plan, first, place, pairs[:1], panels, totals and totals[:1])
            return [ours[0], theirs[0]]

        ours, theirs = get("k", len(KGROUPS) - 1)
        return ours + send(theirs, sibling, "sums")

    return jax.shard_map(
        local,
        mesh=mesh,
        in_specs=(
            P(AXES, None, None),
            P(AXES, None),
            P(AXES),
            P("vblk", None, None, "pair", None),
        ),
        out_specs=P(AXES, None, None),
        check_vma=False,
    )
```

time: 182 us -> 83.2 us (0.46)
  waiting for transfers between devices: 109 us -> 14.6 us
  starting transfers between devices: 8.37 us -> 34 us
  Pallas kernels: 0 us -> 25.3 us
  local copies, waits for them, and re-layouts: 23.7 us -> 3.11 us
  matrix products: 17 us -> 0 us
  between operations: 13.5 us -> 0.25 us
  other arithmetic: 9.76 us -> 5.56 us
    ppermute x4 -> x26, waiting for transfers between devices: 71.4 us -> 14.6 us  [send(): return lax.ppermute(x, AXES, pairs)]
    all_gather x1 -> x0, waiting for transfers between devices: 37.1 us -> none  [local(): whole = lax.all_gather(chol_panel, 'pair', axis=3, tiled=True)]
    ppermute x4 -> x26, starting transfers between devices: 8.37 us -> 34 us  [send(): return lax.ppermute(x, AXES, pairs)]
    pallas_call x0 -> x5, Pallas kernels: none -> 25.3 us  [ladder(): pl.pallas_call(functools.partial(ladder_kernel, plan, chunk, sets, len(pa...]
    dot_general x2 -> x0, matrix products: 17 us -> none  [the longest x1 8.71 us: local(): jnp.einsum('pqik,pqlk->pil', half_product, blocks, preferred_element_type...]
    gather x1 -> x0, local copies, waits for them, and re-layouts: 10 us -> none  [local(): window = jnp.take(neighbourhood, row_index, axis=0)]
    select_n x2 -> x1, other arithmetic: 8.33 us -> 0.01 us  [local(): jnp.where(jnp.arange(8) < 4, jnp.where(jnp.arange(8) == 0, core, jnp.wher...]
    unnamed x6 -> x8, local copies, waits for them, and re-layouts: 7.38 us -> 0.98 us
  transfers between devices with their start and end apart: 5 -> 26, of which waited for: 3 -> 10; matrix products, arithmetic and copies ran while one was open for 5% -> 7% of each run, Pallas kernels for 0% -> 26%
where the time goes in v2:
time: 83.2 us; the launch traced here: 82.8 us
  starting transfers between devices  34 us (41%)
  Pallas kernels  25.3 us (30%)
  waiting for transfers between devices  14.6 us (18%)
  other arithmetic  5.56 us (7%)
  local copies, waits for them, and re-layouts  3.11 us (4%)
    ppermute x26, starting transfers between devices, send(): return lax.ppermute(x, AXES, pairs)  34 us
    pallas_call x5, Pallas kernels, ladder(): pl.pallas_call(functools.partial(ladder_kernel, plan, chunk, sets, len(pa...  25.3 us
    ppermute x26, waiting for transfers between devices, send(): return lax.ppermute(x, AXES, pairs)  14.6 us
    another operation x4, other arithmetic, get(): memo[name] = jnp.stack(([] if OWN_FIRST else [part]) + get('z', j))  2.43 us
  transfers between devices with their start and end apart: 26, of which 10 were waited for; matrix products, arithmetic and copies ran while one was open for 7% of the time, Pallas kernels for 26%

profile of v2, /device:TPU:0, one launch (start us, length us, event | category | flops | bytes accessed | tf_op | source)
XLA Modules:
  0.0 82.8 jit_solution(16847722111064234489)
XLA Ops:
  0.0 1.0 %copy-done = bf16[1,8,5,32,128]{4,3,2,1,0:T(8,128)(2,1)S(1)} copy-done((bf16[1,8,5,32,128]{4,3,2,1,0:T(8,128)(2,1)S(1)}, bf16[1,8,5,32,128]{4,3,2,1,0:T(8,128)(2,1)}, u32[]{:S(2)}) %copy-start) | copy-done | bytes 327704
  1.0 0.5 collective-permute-start
  1.5 0.1 collective-permute-start.7
  1.6 0.9 %collective-permute-done = bf16[4,5,32,128]{3,2,1,0:T(8,128)(2,1)S(1)} collective-permute-done((bf16[4,5,32,128]{3,2,1,0:T(8,128)(2,1)S(1)}, bf16[4,5,32,128]{3,2,1,0:T(8,128)(2,1)S(1)}, u32[]{:S(2)}, u32[]{:S(2)}) %collective-permute-start) | collective-permute-done | bytes 163872 | tf_op jit(solution)/shard_map/give/ppermute | solution.py:143
  2.5 0.7 fusion.3
  3.2 4.0 %collective-permute-start.9 = (bf16[2,1,5,32,128]{4,3,2,0,1:T(8,128)(2,1)S(1)}, bf16[2,1,5,32,128]{4,3,2,0,1:T(8,128)(2,1)S(1)}, u32[]{:S(2)}, u32[]{:S(2)}) collective-permute-start(bf16[2,1,5,32,128]{4,3,2,0,1:T(8,128)(2,1)S(1)} %get-tuple-element.25), channel_id=1, source_target_pairs={{0,2},{1,3},{2,0},{3,1},{4,6},{5,7},{6,4},{7,5},{8,10},{9,11},{10,... | collective-permute-start | bytes 245768 | tf_op jit(solution)/shard_map/z_0/ppermute | solution.py:143
  7.1 1.3 %collective-permute-start.10 = (bf16[2,1,5,32,128]{4,3,2,0,1:T(8,128)(2,1)S(1)}, bf16[2,1,5,32,128]{4,3,2,0,1:T(8,128)(2,1)S(1)}, u32[]{:S(2)}, u32[]{:S(2)}) collective-permute-start(bf16[2,1,5,32,128]{4,3,2,0,1:T(8,128)(2,1)S(1)} %get-tuple-element.25), channel_id=1, source_target_pairs={{0,3},{1,2},{2,1},{3,0},{4,7},{5,6},{6,5},{7,4},{8,11},{9,10},{10,... | collective-permute-start | bytes 245768 | tf_op jit(solution)/shard_map/z_0/ppermute | solution.py:143
  8.5 0.2 collective-permute-start.8
  8.7 1.8 %collective-permute-start.14 = (bf16[2,1,5,32,128]{4,3,2,0,1:T(8,128)(2,1)S(1)}, bf16[2,1,5,32,128]{4,3,2,0,1:T(8,128)(2,1)S(1)}, u32[]{:S(2)}, u32[]{:S(2)}) collective-permute-start(bf16[2,1,5,32,128]{4,3,2,0,1:T(8,128)(2,1)S(1)} %get-tuple-element.26), channel_id=1, source_target_pairs={{0,1},{1,0},{2,3},{3,2},{4,5},{5,4},{6,7},{7,6},{8,9},{9,8},{10,11... | collective-permute-start | bytes 245768 | tf_op jit(solution)/shard_map/z_1/ppermute | solution.py:143
  10.5 0.8 pad_maximum_fusion
  11.3 2.2 %collective-permute-done.9 = bf16[2,1,5,32,128]{4,3,2,0,1:T(8,128)(2,1)S(1)} collective-permute-done((bf16[2,1,5,32,128]{4,3,2,0,1:T(8,128)(2,1)S(1)}, bf16[2,1,5,32,128]{4,3,2,0,1:T(8,128)(2,1)S(1)}, u32[]{:S(2)}, u32[]{:S(2)}) %collective-permute-start.9) | collective-permute-done | bytes 81952 | tf_op jit(solution)/shard_map/z_0/ppermute | solution.py:143
  13.5 0.0 collective-permute-start.15
  13.5 0.8 collective-permute-done.10
  14.3 2.8 %collective-permute-start.16 = (bf16[2,1,5,32,128]{4,3,2,0,1:T(8,128)(2,1)S(1)}, bf16[2,1,5,32,128]{4,3,2,0,1:T(8,128)(2,1)S(1)}, u32[]{:S(2)}, u32[]{:S(2)}) collective-permute-start(bf16[2,1,5,32,128]{4,3,2,0,1:T(8,128)(2,1)S(1)} %get-tuple-element.26), channel_id=1, source_target_pairs={{0,3},{1,2},{2,1},{3,0},{4,7},{5,6},{6,5},{7,4},{8,11},{9,10},{10,... | collective-permute-start | bytes 245768 | tf_op jit(solution)/shard_map/z_1/ppermute | solution.py:143
  17.1 0.0 collective-permute-done.8
  17.1 1.5 %collective-permute-start.1 = (bf16[2,4,5,32,128]{4,3,2,0,1:T(8,128)(2,1)}, bf16[2,4,5,32,128]{4,3,2,0,1:T(8,128)(2,1)}, u32[]{:S(2)}, u32[]{:S(2)}) collective-permute-start(bf16[2,4,5,32,128]{4,3,2,0,1:T(8,128)(2,1)} %pad_maximum_fusion), channel_id=1, source_target_pairs={{0,8},{1,9},{2,10},{3,11},{4,12},{5,13},{6,14},{7,15},{8,0},{9,1},... | collective-permute-start | bytes 983048 | tf_op jit(solution)/shard_map/x_own/ppermute | solution.py:143
  18.6 0.7 pad_maximum_fusion.2
  19.3 0.0 collective-permute-done.14
  19.3 2.0 %collective-permute-start.3 = (bf16[2,1,5,32,128]{4,3,2,0,1:T(8,128)(2,1)}, bf16[2,1,5,32,128]{4,3,2,0,1:T(8,128)(2,1)}, u32[]{:S(2)}, u32[]{:S(2)}) collective-permute-start(bf16[2,1,5,32,128]{4,3,2,0,1:T(8,128)(2,1)} %get-tuple-element.24), channel_id=1, source_target_pairs={{0,1},{1,0},{2,3},{3,2},{4,5},{5,4},{6,7},{7,6},{8,9},{9,8},{10,11... | collective-permute-start | bytes 245768 | tf_op jit(solution)/shard_map/z_3/ppermute | solution.py:143
  21.3 1.7 %collective-permute-done.15 = bf16[2,1,5,32,128]{4,3,2,0,1:T(8,128)(2,1)S(1)} collective-permute-done((bf16[2,1,5,32,128]{4,3,2,0,1:T(8,128)(2,1)S(1)}, bf16[2,1,5,32,128]{4,3,2,0,1:T(8,128)(2,1)S(1)}, u32[]{:S(2)}, u32[]{:S(2)}) %collective-permute-start.15) | collective-permute-done | bytes 81952 | tf_op jit(solution)/shard_map/z_1/ppermute | solution.py:143
  23.0 1.5 %collective-permute-start.11 = (bf16[3,2,1,5,32,128]{5,4,3,1,2,0:T(8,128)(2,1)}, bf16[3,2,1,5,32,128]{5,4,3,1,2,0:T(8,128)(2,1)}, u32[]{:S(2)}, u32[]{:S(2)}) collective-permute-start(bf16[3,2,1,5,32,128]{5,4,3,1,2,0:T(8,128)(2,1)} %get-tuple-element.31), channel_id=1, source_target_pairs={{0,8},{1,9},{2,10},{3,11},{4,12},{5,13},{6,14},{7,15},{8,0},{9,1},... | collective-permute-start | bytes 737288 | tf_op jit(solution)/shard_map/x_0/ppermute | solution.py:143
  24.5 0.0 collective-permute-done.16
  24.5 0.7 pad_maximum_fusion.3
  25.3 0.5 collective-permute-start.17
  25.8 0.1 copy.11
  25.9 0.0 collective-permute-done.3
  25.9 1.3 %collective-permute-start.4 = (bf16[2,1,5,32,128]{4,3,2,0,1:T(8,128)(2,1)}, bf16[2,1,5,32,128]{4,3,2,0,1:T(8,128)(2,1)S(1)}, u32[]{:S(2)}, u32[]{:S(2)}) collective-permute-start(bf16[2,1,5,32,128]{4,3,2,0,1:T(8,128)(2,1)} %get-tuple-element.24), channel_id=1, source_target_pairs={{0,2},{1,3},{2,0},{3,1},{4,6},{5,7},{6,4},{7,5},{8,10},{9,11},{10,... | collective-permute-start | bytes 245768 | tf_op jit(solution)/shard_map/z_3/ppermute | solution.py:143
  27.2 0.8 collective-permute-done.1
  28.0 1.8 %collective-permute-start.5 = (bf16[2,1,5,32,128]{4,3,2,0,1:T(8,128)(2,1)}, bf16[2,1,5,32,128]{4,3,2,0,1:T(8,128)(2,1)S(1)}, u32[]{:S(2)}, u32[]{:S(2)}) collective-permute-start(bf16[2,1,5,32,128]{4,3,2,0,1:T(8,128)(2,1)} %get-tuple-element.24), channel_id=1, source_target_pairs={{0,3},{1,2},{2,1},{3,0},{4,7},{5,6},{6,5},{7,4},{8,11},{9,10},{10,... | collective-permute-start | bytes 245768 | tf_op jit(solution)/shard_map/z_3/ppermute | solution.py:143
  29.8 0.1 pad_add_fusion.refs_1_
  29.9 3.7 %collective-permute-done.4 = bf16[2,1,5,32,128]{4,3,2,0,1:T(8,128)(2,1)S(1)} collective-permute-done((bf16[2,1,5,32,128]{4,3,2,0,1:T(8,128)(2,1)}, bf16[2,1,5,32,128]{4,3,2,0,1:T(8,128)(2,1)S(1)}, u32[]{:S(2)}, u32[]{:S(2)}) %collective-permute-start.4) | collective-permute-done | bytes 81952 | tf_op jit(solution)/shard_map/z_3/ppermute | solution.py:143
  33.6 0.0 collective-permute-start.20
  33.6 1.1 %collective-permute-done.5 = bf16[2,1,5,32,128]{4,3,2,0,1:T(8,128)(2,1)S(1)} collective-permute-done((bf16[2,1,5,32,128]{4,3,2,0,1:T(8,128)(2,1)}, bf16[2,1,5,32,128]{4,3,2,0,1:T(8,128)(2,1)S(1)}, u32[]{:S(2)}, u32[]{:S(2)}) %collective-permute-start.5) | collective-permute-done | bytes 81952 | tf_op jit(solution)/shard_map/z_3/ppermute | solution.py:143
  34.7 3.4 %collective-permute-start.2 = (bf16[2,4,5,32,128]{4,3,2,0,1:T(8,128)(2,1)}, bf16[2,4,5,32,128]{4,3,2,0,1:T(8,128)(2,1)S(1)}, u32[]{:S(2)}, u32[]{:S(2)}) collective-permute-start(bf16[2,4,5,32,128]{4,3,2,0,1:T(8,128)(2,1)} %collective-permute-done.1), channel_id=1, source_target_pairs={{0,16},{1,17},{2,18},{3,19},{4,20},{5,21},{6,22},{7,23},{24,8},{25... | collective-permute-start | bytes 983048 | tf_op jit(solution)/shard_map/y_own/ppermute | solution.py:143
  38.1 0.0 collective-permute-done.11
  38.1 1.3 %collective-permute-start.12 = (bf16[3,2,1,5,32,128]{5,4,3,1,2,0:T(8,128)(2,1)}, bf16[3,2,1,5,32,128]{5,4,3,1,2,0:T(8,128)(2,1)S(1)}, u32[]{:S(2)}, u32[]{:S(2)}) collective-permute-start(bf16[3,2,1,5,32,128]{5,4,3,1,2,0:T(8,128)(2,1)} %collective-permute-done.11), channel_id=1, source_target_pairs={{0,16},{1,17},{2,18},{3,19},{4,20},{5,21},{6,22},{7,23},{24,8},{25... | collective-permute-start | bytes 737288 | tf_op jit(solution)/shard_map/y_0/ppermute | solution.py:143
  39.5 1.0 %copy.33.refs_5_.refs_3_ = bf16[2,4,5,32,128]{4,3,2,1,0:T(8,128)(2,1)S(1)} copy(bf16[2,4,5,32,128]{4,3,2,0,1:T(8,128)(2,1)} %pad_maximum_fusion) | data formatting | bytes 655360 | tf_op jit(solution)/shard_map/stack | solution.py:163
  40.5 0.0 collective-permute-done.17
  40.5 1.5 %collective-permute-start.21 = (bf16[2,1,5,32,128]{4,3,2,0,1:T(8,128)(2,1)S(1)}, bf16[2,1,5,32,128]{4,3,2,0,1:T(8,128)(2,1)S(1)}, u32[]{:S(2)}, u32[]{:S(2)}) collective-permute-start(bf16[2,1,5,32,128]{4,3,2,0,1:T(8,128)(2,1)S(1)} %get-tuple-element.20), channel_id=1, source_target_pairs={{0,2},{1,3},{2,0},{3,1},{4,6},{5,7},{6,4},{7,5},{8,10},{9,11},{10,... | collective-permute-start | bytes 245768 | tf_op jit(solution)/shard_map/z_2/ppermute | solution.py:143
  42.0 0.0 collective-permute-done.20
  42.0 2.1 %collective-permute-start.22 = (bf16[2,1,5,32,128]{4,3,2,0,1:T(8,128)(2,1)S(1)}, bf16[2,1,5,32,128]{4,3,2,0,1:T(8,128)(2,1)S(1)}, u32[]{:S(2)}, u32[]{:S(2)}) collective-permute-start(bf16[2,1,5,32,128]{4,3,2,0,1:T(8,128)(2,1)S(1)} %get-tuple-element.20), channel_id=1, source_target_pairs={{0,3},{1,2},{2,1},{3,0},{4,7},{5,6},{6,5},{7,4},{8,11},{9,10},{10,... | collective-permute-start | bytes 245768 | tf_op jit(solution)/shard_map/z_2/ppermute | solution.py:143
  44.1 0.9 %pad_maximum_fusion.1.refs_6_ = bf16[3,2,1,5,32,128]{5,4,3,2,1,0:T(8,128)(2,1)S(1)} fusion(bf16[1,2,1,5,32,128]{5,4,3,2,1,0:T(8,128)(2,1)S(1)} %bitcast.45, bf16[1,2,1,5,32,128]{5,4,3,2,1,0:T(8,128)(2,1)S(1)} %bitcast.43, bf16[1,2,1,5,32,128]{5,4,3,2,1,0:T(8,128)(2,1)} %bitcast.5), kind=kLoop, calls=%fused_computation.9 | loop fusion | flops 245760 | bytes 491520 | tf_op jit(solution)/shard_map/stack | solution.py:184
  45.0 1.0 %copy.34.refs_6_.refs_4_ = bf16[2,4,5,32,128]{4,3,2,1,0:T(8,128)(2,1)S(1)} copy(bf16[2,4,5,32,128]{4,3,2,0,1:T(8,128)(2,1)} %collective-permute-done.1) | data formatting | bytes 655360 | tf_op jit(solution)/shard_map/x_own/ppermute | solution.py:143
  46.0 0.7 collective-permute-done.21
  46.8 1.6 %collective-permute-done.22 = bf16[2,1,5,32,128]{4,3,2,0,1:T(8,128)(2,1)S(1)} collective-permute-done((bf16[2,1,5,32,128]{4,3,2,0,1:T(8,128)(2,1)S(1)}, bf16[2,1,5,32,128]{4,3,2,0,1:T(8,128)(2,1)S(1)}, u32[]{:S(2)}, u32[]{:S(2)}) %collective-permute-start.22) | collective-permute-done | bytes 81952 | tf_op jit(solution)/shard_map/z_2/ppermute | solution.py:143
  48.3 1.3 %collective-permute-start.18 = (bf16[3,2,1,5,32,128]{5,4,3,1,2,0:T(8,128)(2,1)S(1)}, bf16[3,2,1,5,32,128]{5,4,3,1,2,0:T(8,128)(2,1)S(1)}, u32[]{:S(2)}, u32[]{:S(2)}) collective-permute-start(bf16[3,2,1,5,32,128]{5,4,3,1,2,0:T(8,128)(2,1)S(1)} %collective-permute-done.17), channel_id=1, source_target_pairs={{0,16},{1,17},{2,18},{3,19},{4,20},{5,21},{6,22},{7,23},{24,8},{25... | collective-permute-start | bytes 737288 | tf_op jit(solution)/shard_map/y_1/ppermute | solution.py:143
  49.7 0.1 collective-permute-start.23
  49.8 0.0 collective-permute-done.12
  49.9 6.3 %shard_map.46 = (f32[4,384,384]{2,1,0:T(8,128)S(1)}, f32[4,384,384]{2,1,0:T(8,128)S(1)}) custom-call(s32[8]{0:T(128)S(1)} %compare_select_fusion.3.refs_0_, s32[4,4]{1,0:T(4,128)S(1)} %pad_add_fusion.refs_1_, s32[4,4]{1,0:T(4,128)S(1)} %collective-permute-done.6.refs_2_.refs_1_, bf16[4,384,384]{2,1,0:T(8,128)(2,1)S(1)} %copy-done.1, ...), custom_call_target="tpu_custom_call" | custom-call | flops 1811939328 | bytes 8388608 | tf_op jit(solution)/shard_map/pallas_call | solution.py:100
  56.2 2.1 %collective-permute-start.13 = (bf16[3,2,1,5,32,128]{5,4,3,2,1,0:T(8,128)(2,1)S(1)}, bf16[3,2,1,5,32,128]{5,4,3,2,1,0:T(8,128)(2,1)S(1)}, u32[]{:S(2)}, u32[]{:S(2)}) collective-permute-start(bf16[3,2,1,5,32,128]{5,4,3,2,1,0:T(8,128)(2,1)S(1)} %pad_maximum_fusion.1.refs_6_), channel_id=1, source_target_pairs={{0,8},{1,9},{2,10},{3,11},{4,12},{5,13},{6,14},{7,15},{8,0},{9,1},... | collective-permute-start | bytes 737288 | tf_op jit(solution)/shard_map/x_3/ppermute | solution.py:143
  58.2 0.0 collective-permute-done.23
  58.2 1.4 %collective-permute-start.24 = (bf16[3,2,1,5,32,128]{5,4,3,1,2,0:T(8,128)(2,1)S(1)}, bf16[3,2,1,5,32,128]{5,4,3,1,2,0:T(8,128)(2,1)S(1)}, u32[]{:S(2)}, u32[]{:S(2)}) collective-permute-start(bf16[3,2,1,5,32,128]{5,4,3,1,2,0:T(8,128)(2,1)S(1)} %collective-permute-done.23), channel_id=1, source_target_pairs={{0,16},{1,17},{2,18},{3,19},{4,20},{5,21},{6,22},{7,23},{24,8},{25... | collective-permute-start | bytes 737288 | tf_op jit(solution)/shard_map/y_2/ppermute | solution.py:143
  59.6 0.0 collective-permute-done.18
  59.6 6.1 %shard_map.47 = (f32[4,384,384]{2,1,0:T(8,128)S(1)}, f32[4,384,384]{2,1,0:T(8,128)S(1)}) custom-call(s32[8]{0:T(128)S(1)} %compare_select_fusion.3.refs_0_, s32[4,4]{1,0:T(4,128)S(1)} %pad_add_fusion.refs_1_, s32[4,4]{1,0:T(4,128)S(1)} %collective-permute-done.6.refs_2_.refs_1_, ...), custom_call_target="tpu_custom_call", output_to_operand_aliasing={{0}: (11, {}), {1}: (12, {})} | custom-call | flops 1811939328 | bytes 8388608 | tf_op jit(solution)/shard_map/pallas_call | solution.py:100
  65.7 0.0 collective-permute-done.13.refs_7_
  65.7 1.3 %collective-permute-start.19 = (bf16[3,2,1,5,32,128]{5,4,3,2,1,0:T(8,128)(2,1)S(1)}, bf16[3,2,1,5,32,128]{5,4,3,2,1,0:T(8,128)(2,1)S(1)}, u32[]{:S(2)}, u32[]{:S(2)}) collective-permute-start(bf16[3,2,1,5,32,128]{5,4,3,2,1,0:T(8,128)(2,1)S(1)} %collective-permute-done.13.refs_7_), channel_id=1, source_target_pairs={{0,16},{1,17},{2,18},{3,19},{4,20},{5,21},{6,22},{7,23},{24,8},{25... | collective-permute-start | bytes 737288 | tf_op jit(solution)/shard_map/y_3/ppermute | solution.py:143
  67.0 0.0 collective-permute-done.24
  67.0 6.1 %shard_map.48 = (f32[4,384,384]{2,1,0:T(8,128)S(1)}, f32[4,384,384]{2,1,0:T(8,128)S(1)}) custom-call(s32[8]{0:T(128)S(1)} %compare_select_fusion.3.refs_0_, s32[4,4]{1,0:T(4,128)S(1)} %pad_add_fusion.refs_1_, s32[4,4]{1,0:T(4,128)S(1)} %collective-permute-done.6.refs_2_.refs_1_, ...), custom_call_target="tpu_custom_call", output_to_operand_aliasing={{0}: (11, {}), {1}: (12, {})} | custom-call | flops 1811939328 | bytes 8388608 | tf_op jit(solution)/shard_map/pallas_call | solution.py:100
  73.1 0.0 collective-permute-done.19.refs_8_
  73.1 3.4 %shard_map.50 = f32[4,384,384]{2,1,0:T(8,128)S(1)} custom-call(s32[8]{0:T(128)S(1)} %compare_select_fusion.3.refs_0_, s32[4,4]{1,0:T(4,128)S(1)} %collective-permute-done.6.refs_2_.refs_1_, bf16[4,384,384]{2,1,0:T(8,128)(2,1)S(1)} %collective-permute-done.7.refs_4_.refs_2_, ...), custom_call_target="tpu_custom_call", output_to_operand_aliasing={{}: (9, {})} | custom-call | flops 905969664 | bytes 8388608 | tf_op jit(solution)/shard_map/pallas_call | solution.py:100
  76.6 0.1 collective-permute-start.25
  76.7 3.4 %shard_map.49 = f32[4,384,384]{2,1,0:T(8,128)S(1)} custom-call(s32[8]{0:T(128)S(1)} %compare_select_fusion.3.refs_0_, s32[4,4]{1,0:T(4,128)S(1)} %pad_add_fusion.refs_1_, bf16[4,384,384]{2,1,0:T(8,128)(2,1)S(1)} %copy-done.1, bf16[2,4,5,32,128]{4,3,2,1,0:T(8,128)(2,1)S(1)} %copy.33.refs_5_.refs_3_, ...), custom_call_target="tpu_custom_call", output_to_operand_aliasing={{}: (9, {})} | custom-call | flops 905969664 | bytes 8388608 | tf_op jit(solution)/shard_map/pallas_call | solution.py:100
  80.1 1.1 %collective-permute-done.25 = f32[4,384,384]{2,1,0:T(8,128)S(1)} collective-permute-done((f32[4,384,384]{2,1,0:T(8,128)S(1)}, f32[4,384,384]{2,1,0:T(8,128)S(1)}, u32[]{:S(2)}, u32[]{:S(2)}) %collective-permute-start.25) | collective-permute-done | bytes 2359328 | tf_op jit(solution)/shard_map/sums/ppermute | solution.py:143
  81.2 1.6 %add.16 = f32[4,384,384]{2,1,0:T(8,128)} add(f32[4,384,384]{2,1,0:T(8,128)S(1)} %shard_map.49, f32[4,384,384]{2,1,0:T(8,128)S(1)} %collective-permute-done.25) | non-fusion elementwise | flops 589824 | bytes 7077888 | tf_op jit(solution)/shard_map/add | solution.py:226
  (17 shorter events, 0.1 us)
Async XLA Ops:
  0.0 1.0 %copy-start = (bf16[1,8,5,32,128]{4,3,2,1,0:T(8,128)(2,1)S(1)}, bf16[1,8,5,32,128]{4,3,2,1,0:T(8,128)(2,1)}, u32[]{:S(2)}) copy-start(bf16[1,8,5,32,128]{4,3,2,1,0:T(8,128)(2,1)} %param.7) | copy-start | bytes 983044
  0.0 25.8 %copy-start.3 = (s32[4]{0:T(128)S(1)}, s32[4]{0:T(128)}, u32[]{:S(2)}) copy-start(s32[4]{0:T(128)} %param.6) | copy-start | bytes 52
  0.0 29.8 %copy-start.2 = (s32[4,3]{1,0:T(4,128)S(1)}, s32[4,3]{1,0:T(4,128)}, u32[]{:S(2)}) copy-start(s32[4,3]{1,0:T(4,128)} %param.5) | copy-start | bytes 148
  1.0 1.5 %collective-permute-start = (bf16[4,5,32,128]{3,2,1,0:T(8,128)(2,1)S(1)}, bf16[4,5,32,128]{3,2,1,0:T(8,128)(2,1)S(1)}, u32[]{:S(2)}, u32[]{:S(2)}) collective-permute-start(bf16[4,5,32,128]{3,2,1,0:T(8,128)(2,1)S(1)} %dynamic-slice_bitcast_fusion), channel_id=1, source_target_pairs={{0,4},{1,5},{2,6},{3,7},{4,0},{5,1},{6,2},{7,3},{8,12},{9,13},{10,... | collective-permute-start | bytes 491528 | tf_op jit(solution)/shard_map/give/ppermute | solution.py:143
  1.5 48.3 %collective-permute-start.7 = (bf16[4,384,384]{2,1,0:T(8,128)(2,1)}, bf16[4,384,384]{2,1,0:T(8,128)(2,1)S(1)}, u32[]{:S(2)}, u32[]{:S(2)}) collective-permute-start(bf16[4,384,384]{2,1,0:T(8,128)(2,1)} %refs_2_.1), channel_id=1, source_target_pairs={{0,4},{1,5},{2,6},{3,7},{4,0},{5,1},{6,2},{7,3},{8,12},{9,13},{10,... | collective-permute-start | bytes 3538952 | tf_op jit(solution)/shard_map/p_far/ppermute | solution.py:143
  3.2 10.3 %collective-permute-start.9 = (bf16[2,1,5,32,128]{4,3,2,0,1:T(8,128)(2,1)S(1)}, bf16[2,1,5,32,128]{4,3,2,0,1:T(8,128)(2,1)S(1)}, u32[]{:S(2)}, u32[]{:S(2)}) collective-permute-start(bf16[2,1,5,32,128]{4,3,2,0,1:T(8,128)(2,1)S(1)} %get-tuple-element.25), channel_id=1, source_target_pairs={{0,2},{1,3},{2,0},{3,1},{4,6},{5,7},{6,4},{7,5},{8,10},{9,11},{10,... | collective-permute-start | bytes 245768 | tf_op jit(solution)/shard_map/z_0/ppermute | solution.py:143
  7.1 7.1 %collective-permute-start.10 = (bf16[2,1,5,32,128]{4,3,2,0,1:T(8,128)(2,1)S(1)}, bf16[2,1,5,32,128]{4,3,2,0,1:T(8,128)(2,1)S(1)}, u32[]{:S(2)}, u32[]{:S(2)}) collective-permute-start(bf16[2,1,5,32,128]{4,3,2,0,1:T(8,128)(2,1)S(1)} %get-tuple-element.25), channel_id=1, source_target_pairs={{0,3},{1,2},{2,1},{3,0},{4,7},{5,6},{6,5},{7,4},{8,11},{9,10},{10,... | collective-permute-start | bytes 245768 | tf_op jit(solution)/shard_map/z_0/ppermute | solution.py:143
  8.5 8.6 %collective-permute-start.8 = (bf16[2,1,5,32,128]{4,3,2,0,1:T(8,128)(2,1)S(1)}, bf16[2,1,5,32,128]{4,3,2,0,1:T(8,128)(2,1)S(1)}, u32[]{:S(2)}, u32[]{:S(2)}) collective-permute-start(bf16[2,1,5,32,128]{4,3,2,0,1:T(8,128)(2,1)S(1)} %get-tuple-element.25), channel_id=1, source_target_pairs={{0,1},{1,0},{2,3},{3,2},{4,5},{5,4},{6,7},{7,6},{8,9},{9,8},{10,11... | collective-permute-start | bytes 245768 | tf_op jit(solution)/shard_map/z_0/ppermute | solution.py:143
  8.7 10.6 %collective-permute-start.14 = (bf16[2,1,5,32,128]{4,3,2,0,1:T(8,128)(2,1)S(1)}, bf16[2,1,5,32,128]{4,3,2,0,1:T(8,128)(2,1)S(1)}, u32[]{:S(2)}, u32[]{:S(2)}) collective-permute-start(bf16[2,1,5,32,128]{4,3,2,0,1:T(8,128)(2,1)S(1)} %get-tuple-element.26), channel_id=1, source_target_pairs={{0,1},{1,0},{2,3},{3,2},{4,5},{5,4},{6,7},{7,6},{8,9},{9,8},{10,11... | collective-permute-start | bytes 245768 | tf_op jit(solution)/shard_map/z_1/ppermute | solution.py:143
  13.5 9.6 %collective-permute-start.15 = (bf16[2,1,5,32,128]{4,3,2,0,1:T(8,128)(2,1)S(1)}, bf16[2,1,5,32,128]{4,3,2,0,1:T(8,128)(2,1)S(1)}, u32[]{:S(2)}, u32[]{:S(2)}) collective-permute-start(bf16[2,1,5,32,128]{4,3,2,0,1:T(8,128)(2,1)S(1)} %get-tuple-element.26), channel_id=1, source_target_pairs={{0,2},{1,3},{2,0},{3,1},{4,6},{5,7},{6,4},{7,5},{8,10},{9,11},{10,... | collective-permute-start | bytes 245768 | tf_op jit(solution)/shard_map/z_1/ppermute | solution.py:143
  14.3 10.3 %collective-permute-start.16 = (bf16[2,1,5,32,128]{4,3,2,0,1:T(8,128)(2,1)S(1)}, bf16[2,1,5,32,128]{4,3,2,0,1:T(8,128)(2,1)S(1)}, u32[]{:S(2)}, u32[]{:S(2)}) collective-permute-start(bf16[2,1,5,32,128]{4,3,2,0,1:T(8,128)(2,1)S(1)} %get-tuple-element.26), channel_id=1, source_target_pairs={{0,3},{1,2},{2,1},{3,0},{4,7},{5,6},{6,5},{7,4},{8,11},{9,10},{10,... | collective-permute-start | bytes 245768 | tf_op jit(solution)/shard_map/z_1/ppermute | solution.py:143
  17.1 10.9 %collective-permute-start.1 = (bf16[2,4,5,32,128]{4,3,2,0,1:T(8,128)(2,1)}, bf16[2,4,5,32,128]{4,3,2,0,1:T(8,128)(2,1)}, u32[]{:S(2)}, u32[]{:S(2)}) collective-permute-start(bf16[2,4,5,32,128]{4,3,2,0,1:T(8,128)(2,1)} %pad_maximum_fusion), channel_id=1, source_target_pairs={{0,8},{1,9},{2,10},{3,11},{4,12},{5,13},{6,14},{7,15},{8,0},{9,1},... | collective-permute-start | bytes 983048 | tf_op jit(solution)/shard_map/x_own/ppermute | solution.py:143
  18.6 31.3 %copy-start.1 = (bf16[4,384,384]{2,1,0:T(8,128)(2,1)S(1)}, bf16[4,384,384]{2,1,0:T(8,128)(2,1)}, u32[]{:S(2)}) copy-start(bf16[4,384,384]{2,1,0:T(8,128)(2,1)} %refs_2_.1) | copy-start | bytes 3538948
  19.3 6.6 %collective-permute-start.3 = (bf16[2,1,5,32,128]{4,3,2,0,1:T(8,128)(2,1)}, bf16[2,1,5,32,128]{4,3,2,0,1:T(8,128)(2,1)}, u32[]{:S(2)}, u32[]{:S(2)}) collective-permute-start(bf16[2,1,5,32,128]{4,3,2,0,1:T(8,128)(2,1)} %get-tuple-element.24), channel_id=1, source_target_pairs={{0,1},{1,0},{2,3},{3,2},{4,5},{5,4},{6,7},{7,6},{8,9},{9,8},{10,11... | collective-permute-start | bytes 245768 | tf_op jit(solution)/shard_map/z_3/ppermute | solution.py:143
  23.0 15.1 %collective-permute-start.11 = (bf16[3,2,1,5,32,128]{5,4,3,1,2,0:T(8,128)(2,1)}, bf16[3,2,1,5,32,128]{5,4,3,1,2,0:T(8,128)(2,1)}, u32[]{:S(2)}, u32[]{:S(2)}) collective-permute-start(bf16[3,2,1,5,32,128]{5,4,3,1,2,0:T(8,128)(2,1)} %get-tuple-element.31), channel_id=1, source_target_pairs={{0,8},{1,9},{2,10},{3,11},{4,12},{5,13},{6,14},{7,15},{8,0},{9,1},... | collective-permute-start | bytes 737288 | tf_op jit(solution)/shard_map/x_0/ppermute | solution.py:143
  25.3 15.2 %collective-permute-start.17 = (bf16[3,2,1,5,32,128]{5,4,3,1,2,0:T(8,128)(2,1)}, bf16[3,2,1,5,32,128]{5,4,3,1,2,0:T(8,128)(2,1)S(1)}, u32[]{:S(2)}, u32[]{:S(2)}) collective-permute-start(bf16[3,2,1,5,32,128]{5,4,3,1,2,0:T(8,128)(2,1)} %get-tuple-element.29), channel_id=1, source_target_pairs={{0,8},{1,9},{2,10},{3,11},{4,12},{5,13},{6,14},{7,15},{8,0},{9,1},... | collective-permute-start | bytes 737288 | tf_op jit(solution)/shard_map/x_1/ppermute | solution.py:143
  25.9 7.7 %collective-permute-start.4 = (bf16[2,1,5,32,128]{4,3,2,0,1:T(8,128)(2,1)}, bf16[2,1,5,32,128]{4,3,2,0,1:T(8,128)(2,1)S(1)}, u32[]{:S(2)}, u32[]{:S(2)}) collective-permute-start(bf16[2,1,5,32,128]{4,3,2,0,1:T(8,128)(2,1)} %get-tuple-element.24), channel_id=1, source_target_pairs={{0,2},{1,3},{2,0},{3,1},{4,6},{5,7},{6,4},{7,5},{8,10},{9,11},{10,... | collective-permute-start | bytes 245768 | tf_op jit(solution)/shard_map/z_3/ppermute | solution.py:143
  28.0 6.7 %collective-permute-start.5 = (bf16[2,1,5,32,128]{4,3,2,0,1:T(8,128)(2,1)}, bf16[2,1,5,32,128]{4,3,2,0,1:T(8,128)(2,1)S(1)}, u32[]{:S(2)}, u32[]{:S(2)}) collective-permute-start(bf16[2,1,5,32,128]{4,3,2,0,1:T(8,128)(2,1)} %get-tuple-element.24), channel_id=1, source_target_pairs={{0,3},{1,2},{2,1},{3,0},{4,7},{5,6},{6,5},{7,4},{8,11},{9,10},{10,... | collective-permute-start | bytes 245768 | tf_op jit(solution)/shard_map/z_3/ppermute | solution.py:143
  33.6 8.4 %collective-permute-start.20 = (bf16[2,1,5,32,128]{4,3,2,0,1:T(8,128)(2,1)S(1)}, bf16[2,1,5,32,128]{4,3,2,0,1:T(8,128)(2,1)S(1)}, u32[]{:S(2)}, u32[]{:S(2)}) collective-permute-start(bf16[2,1,5,32,128]{4,3,2,0,1:T(8,128)(2,1)S(1)} %get-tuple-element.20), channel_id=1, source_target_pairs={{0,1},{1,0},{2,3},{3,2},{4,5},{5,4},{6,7},{7,6},{8,9},{9,8},{10,11... | collective-permute-start | bytes 245768 | tf_op jit(solution)/shard_map/z_2/ppermute | solution.py:143
  34.7 15.0 %collective-permute-start.2 = (bf16[2,4,5,32,128]{4,3,2,0,1:T(8,128)(2,1)}, bf16[2,4,5,32,128]{4,3,2,0,1:T(8,128)(2,1)S(1)}, u32[]{:S(2)}, u32[]{:S(2)}) collective-permute-start(bf16[2,4,5,32,128]{4,3,2,0,1:T(8,128)(2,1)} %collective-permute-done.1), channel_id=1, source_target_pairs={{0,16},{1,17},{2,18},{3,19},{4,20},{5,21},{6,22},{7,23},{24,8},{25... | collective-permute-start | bytes 983048 | tf_op jit(solution)/shard_map/y_own/ppermute | solution.py:143
  38.1 11.7 %collective-permute-start.12 = (bf16[3,2,1,5,32,128]{5,4,3,1,2,0:T(8,128)(2,1)}, bf16[3,2,1,5,32,128]{5,4,3,1,2,0:T(8,128)(2,1)S(1)}, u32[]{:S(2)}, u32[]{:S(2)}) collective-permute-start(bf16[3,2,1,5,32,128]{5,4,3,1,2,0:T(8,128)(2,1)} %collective-permute-done.11), channel_id=1, source_target_pairs={{0,16},{1,17},{2,18},{3,19},{4,20},{5,21},{6,22},{7,23},{24,8},{25... | collective-permute-start | bytes 737288 | tf_op jit(solution)/shard_map/y_0/ppermute | solution.py:143
  40.5 6.3 %collective-permute-start.21 = (bf16[2,1,5,32,128]{4,3,2,0,1:T(8,128)(2,1)S(1)}, bf16[2,1,5,32,128]{4,3,2,0,1:T(8,128)(2,1)S(1)}, u32[]{:S(2)}, u32[]{:S(2)}) collective-permute-start(bf16[2,1,5,32,128]{4,3,2,0,1:T(8,128)(2,1)S(1)} %get-tuple-element.20), channel_id=1, source_target_pairs={{0,2},{1,3},{2,0},{3,1},{4,6},{5,7},{6,4},{7,5},{8,10},{9,11},{10,... | collective-permute-start | bytes 245768 | tf_op jit(solution)/shard_map/z_2/ppermute | solution.py:143
  42.0 6.3 %collective-permute-start.22 = (bf16[2,1,5,32,128]{4,3,2,0,1:T(8,128)(2,1)S(1)}, bf16[2,1,5,32,128]{4,3,2,0,1:T(8,128)(2,1)S(1)}, u32[]{:S(2)}, u32[]{:S(2)}) collective-permute-start(bf16[2,1,5,32,128]{4,3,2,0,1:T(8,128)(2,1)S(1)} %get-tuple-element.20), channel_id=1, source_target_pairs={{0,3},{1,2},{2,1},{3,0},{4,7},{5,6},{6,5},{7,4},{8,11},{9,10},{10,... | collective-permute-start | bytes 245768 | tf_op jit(solution)/shard_map/z_2/ppermute | solution.py:143
  46.8 3.1 %collective-permute-start.6 = (s32[4,4]{1,0:T(4,128)S(1)}, s32[4,4]{1,0:T(4,128)S(1)}, u32[]{:S(2)}, u32[]{:S(2)}) collective-permute-start(s32[4,4]{1,0:T(4,128)S(1)} %pad_add_fusion.refs_1_), channel_id=1, source_target_pairs={{0,4},{1,5},{2,6},{3,7},{4,0},{5,1},{6,2},{7,3},{8,12},{9,13},{10,... | collective-permute-start | bytes 200 | tf_op jit(solution)/shard_map/p_info/ppermute | solution.py:143
  48.3 11.3 %collective-permute-start.18 = (bf16[3,2,1,5,32,128]{5,4,3,1,2,0:T(8,128)(2,1)S(1)}, bf16[3,2,1,5,32,128]{5,4,3,1,2,0:T(8,128)(2,1)S(1)}, u32[]{:S(2)}, u32[]{:S(2)}) collective-permute-start(bf16[3,2,1,5,32,128]{5,4,3,1,2,0:T(8,128)(2,1)S(1)} %collective-permute-done.17), channel_id=1, source_target_pairs={{0,16},{1,17},{2,18},{3,19},{4,20},{5,21},{6,22},{7,23},{24,8},{25... | collective-permute-start | bytes 737288 | tf_op jit(solution)/shard_map/y_1/ppermute | solution.py:143
  49.7 8.5 %collective-permute-start.23 = (bf16[3,2,1,5,32,128]{5,4,3,1,2,0:T(8,128)(2,1)S(1)}, bf16[3,2,1,5,32,128]{5,4,3,1,2,0:T(8,128)(2,1)S(1)}, u32[]{:S(2)}, u32[]{:S(2)}) collective-permute-start(bf16[3,2,1,5,32,128]{5,4,3,1,2,0:T(8,128)(2,1)S(1)} %get-tuple-element.27), channel_id=1, source_target_pairs={{0,8},{1,9},{2,10},{3,11},{4,12},{5,13},{6,14},{7,15},{8,0},{9,1},... | collective-permute-start | bytes 737288 | tf_op jit(solution)/shard_map/x_2/ppermute | solution.py:143
  56.2 9.6 %collective-permute-start.13 = (bf16[3,2,1,5,32,128]{5,4,3,2,1,0:T(8,128)(2,1)S(1)}, bf16[3,2,1,5,32,128]{5,4,3,2,1,0:T(8,128)(2,1)S(1)}, u32[]{:S(2)}, u32[]{:S(2)}) collective-permute-start(bf16[3,2,1,5,32,128]{5,4,3,2,1,0:T(8,128)(2,1)S(1)} %pad_maximum_fusion.1.refs_6_), channel_id=1, source_target_pairs={{0,8},{1,9},{2,10},{3,11},{4,12},{5,13},{6,14},{7,15},{8,0},{9,1},... | collective-permute-start | bytes 737288 | tf_op jit(solution)/shard_map/x_3/ppermute | solution.py:143
  58.2 8.8 %collective-permute-start.24 = (bf16[3,2,1,5,32,128]{5,4,3,1,2,0:T(8,128)(2,1)S(1)}, bf16[3,2,1,5,32,128]{5,4,3,1,2,0:T(8,128)(2,1)S(1)}, u32[]{:S(2)}, u32[]{:S(2)}) collective-permute-start(bf16[3,2,1,5,32,128]{5,4,3,1,2,0:T(8,128)(2,1)S(1)} %collective-permute-done.23), channel_id=1, source_target_pairs={{0,16},{1,17},{2,18},{3,19},{4,20},{5,21},{6,22},{7,23},{24,8},{25... | collective-permute-start | bytes 737288 | tf_op jit(solution)/shard_map/y_2/ppermute | solution.py:143
  65.7 7.4 %collective-permute-start.19 = (bf16[3,2,1,5,32,128]{5,4,3,2,1,0:T(8,128)(2,1)S(1)}, bf16[3,2,1,5,32,128]{5,4,3,2,1,0:T(8,128)(2,1)S(1)}, u32[]{:S(2)}, u32[]{:S(2)}) collective-permute-start(bf16[3,2,1,5,32,128]{5,4,3,2,1,0:T(8,128)(2,1)S(1)} %collective-permute-done.13.refs_7_), channel_id=1, source_target_pairs={{0,16},{1,17},{2,18},{3,19},{4,20},{5,21},{6,22},{7,23},{24,8},{25... | collective-permute-start | bytes 737288 | tf_op jit(solution)/shard_map/y_3/ppermute | solution.py:143
  76.6 4.6 %collective-permute-start.25 = (f32[4,384,384]{2,1,0:T(8,128)S(1)}, f32[4,384,384]{2,1,0:T(8,128)S(1)}, u32[]{:S(2)}, u32[]{:S(2)}) collective-permute-start(f32[4,384,384]{2,1,0:T(8,128)S(1)} %shard_map.50), channel_id=1, source_target_pairs={{0,4},{1,5},{2,6},{3,7},{4,0},{5,1},{6,2},{7,3},{8,12},{9,13},{10,... | collective-permute-start | bytes 7077896 | tf_op jit(solution)/shard_map/sums/ppermute | solution.py:143

commit v3 on v2

--- a/solution.py
+++ b/solution.py
@@ -25,67 +25,71 @@
     panel_refs = [refs.pop(0) for _ in range(npanel)]
     sum_refs = [refs.pop(0) for _ in range(sets)] if has_sum else []
     out_refs = [refs.pop(0) for _ in range(sets)]
-    tiles, strips, halves, sem = refs
+    (tiles,) = refs
     core = place_ref[0]
 
-    copies = []
     for i, group, slot, row0, source, first, size in plan:
         shard = panel_refs[i]
         rows = shard.shape[-2]
         row = pl.multiple_of(place_ref[4 + row0] * rows, rows)
-        at = pl.multiple_of(2 * place_ref[1 + group], 2)
-        view = shard.at[:, pl.ds(source, size)] if slot is None else shard.at[slot, :, pl.ds(source, size)]
-        copies.append(
-            pltpu.make_async_copy(
-                view, tiles.at[pl.ds(at, 2), pl.ds(first, size), :, pl.ds(row, rows), :], sem.at[len(copies)]
-            )
-        )
-    for copy in copies:
-        copy.start()
-    for copy in copies:
-        copy.wait()
+        at = 2 * place_ref[1 + group]
+        for k in range(2):
+            for j in range(size):
+                piece = shard[k, source + j] if slot is None else shard[slot, k, source + j]
+                tiles[at + k, first + j, :, pl.ds(row, rows), :] = piece
 
     for k in range(sets):
         info_ref, amp_ref, out_ref = info_refs[k], amp_refs[k], out_refs[k]
 
         @pl.loop(0, amp_ref.shape[0])
         def _(p):
-            rel = info_ref[p, 0]
-            live = [info_ref[p, 1 + a] > 0 for a in range(DW)]
-            masked = jnp.concatenate(
-                [
-                    jnp.concatenate(
-                        [
-                            jnp.where(live[a] & live[b], amp_ref[p, pl.ds(a * VB, VB), pl.ds(b * VB, VB)], 0)
-                            for b in range(DW)
-                        ],
-                        axis=1,
+            live = [jnp.where(info_ref[p, 1 + a] > 0, 1, 0) for a in (0, DW - 1)]
+            count = live[0] + 1 + live[1]
+            start = 1 - live[0]
+
+            def blank(block):
+                dead = pl.ds(pl.multiple_of(block * VB, VB), VB)
+                out_ref[p, dead, :] = jnp.zeros((VB, DW * VB), jnp.float32)
+                out_ref[p, :, dead] = jnp.zeros((DW * VB, VB), jnp.float32)
+
+            for n in range(1, DW + 1):
+
+                @pl.when(count == n)
+                def _():
+                    first = start if n < DW else 0
+                    d = info_ref[p, 0] + first
+                    here = pl.ds(pl.multiple_of(first * VB, VB), n * VB) if n < DW else slice(None)
+                    amps = amp_ref[p, here, here]
+                    blocks = [
+                        jnp.concatenate(
+                            [
+                                jnp.concatenate(
+                                    [tiles[jnp.bitwise_xor(d + a, core), j, b - a + DW - 1] for b in range(n)],
+                                    axis=1,
+                                )
+                                for a in range(n)
+                            ],
+                            axis=0,
+                        )
+                        for j in range(chunk)
+                    ]
+                    halves = [
+                        jnp.dot(x, amps, preferred_element_type=jnp.float32).astype(jnp.bfloat16) for x in blocks
+                    ]
+                    ladder = lax.dot_general(
+                        jnp.concatenate(halves, axis=1),
+                        jnp.concatenate(blocks, axis=1),
+                        (((1,), (1,)), ((), ())),
+                        preferred_element_type=jnp.float32,
                     )
-                    for a in range(DW)
-                ],
-                axis=0,
-            ).astype(jnp.bfloat16)
-            for j in range(chunk):
-                for a in range(DW):
-                    d = jnp.bitwise_xor(rel + a, core)
-                    strips[pl.ds(a * VB, VB), pl.ds(j * DW * VB, DW * VB)] = jnp.concatenate(
-                        [tiles[d, j, b - a + DW - 1] for b in range(DW)], axis=1
-                    )
-            for j in range(chunk):
-                cols = pl.ds(j * DW * VB, DW * VB)
-                halves[:, cols] = jnp.dot(
-                    strips[:, cols], masked, preferred_element_type=jnp.float32
-                ).astype(jnp.bfloat16)
-            ladder = lax.dot_general(
-                halves[...], strips[...], (((1,), (1,)), ((), ())), preferred_element_type=jnp.float32
-            )
-            for a in range(DW):
-                for b in range(DW):
-                    at = (p, pl.ds(a * VB, VB), pl.ds(b * VB, VB))
-                    part = ladder[a * VB : (a + 1) * VB, b * VB : (b + 1) * VB]
                     if has_sum:
-                        part = part + sum_refs[k][at]
-                    out_ref[at] = jnp.where(live[a] & live[b], part, 0.0)
+                        ladder = ladder + sum_refs[k][p, here, here]
+                    out_ref[p, here, here] = ladder
+                    if n == 1:
+                        blank(0)
+                        blank(DW - 1)
+                    if n == 2:
+                        blank(jnp.where(live[0] > 0, DW - 1, 0))
 
 
 def ladder(plan, chunk, place, pairs, panels, totals):
@@ -104,12 +108,9 @@
         out_specs=[vmem] * sets,
         scratch_shapes=[
             pltpu.VMEM((PANELS, chunk, offs, VB, vb), jnp.bfloat16),
-            pltpu.VMEM((width, chunk * width), jnp.bfloat16),
-            pltpu.VMEM((width, chunk * width), jnp.bfloat16),
-            pltpu.SemaphoreType.DMA((len(plan),)),
         ],
         input_output_aliases={at + k: k for k in range(len(totals))},
-        compiler_params=pltpu.CompilerParams(vmem_limit_bytes=24 << 20),
+        compiler_params=pltpu.CompilerParams(vmem_limit_bytes=16 << 20),
         cost_estimate=pl.CostEstimate(
             flops=sets * npair * chunk * 4 * width**3, bytes_accessed=8 << 20, transcendentals=0
         ),

time: 83.2 us -> 77.7 us (0.934)
  Pallas kernels: 25.3 us -> 16.5 us
  starting transfers between devices: 34 us -> 35.9 us
  waiting for transfers between devices: 14.6 us -> 16.1 us
    pallas_call x5, Pallas kernels: 25.3 us -> 16.5 us  [ladder(): pl.pallas_call(functools.partial(ladder_kernel, plan, chunk, sets, len(pa...]
    ppermute x26, starting transfers between devices: 34 us -> 35.9 us  [send(): return lax.ppermute(x, AXES, pairs)]
    ppermute x26, waiting for transfers between devices: 14.6 us -> 16.1 us  [send(): return lax.ppermute(x, AXES, pairs)]
  transfers between devices with their start and end apart: 26 -> 26, of which waited for: 10 -> 11; matrix products, arithmetic and copies ran while one was open for 7% -> 8% of each run, Pallas kernels for 26% -> 18%
where the time goes in v3:
time: 77.7 us; the launch traced here: 77.5 us
  starting transfers between devices  35.9 us (46%)
  Pallas kernels  16.5 us (21%)
  waiting for transfers between devices  16.1 us (21%)
  other arithmetic  5.56 us (7%)
  local copies, waits for them, and re-layouts  3.11 us (4%)
    ppermute x26, starting transfers between devices, send(): return lax.ppermute(x, AXES, pairs)  35.9 us
    pallas_call x5, Pallas kernels, ladder(): pl.pallas_call(functools.partial(ladder_kernel, plan, chunk, sets, len(pa...  16.5 us
    ppermute x26, waiting for transfers between devices, send(): return lax.ppermute(x, AXES, pairs)  16.1 us
    another operation x4, other arithmetic, get(): memo[name] = jnp.stack(([] if OWN_FIRST else [part]) + get('z', j))  2.43 us
    add x1, other arithmetic, local(): return ours + send(theirs, sibling, 'sums')  1.64 us
  transfers between devices with their start and end apart: 26, of which 11 were waited for; matrix products, arithmetic and copies ran while one was open for 8% of the time, Pallas kernels for 18%

profile of v3, /device:TPU:0, one launch (start us, length us, event | category | flops | bytes accessed | tf_op | source)
XLA Modules:
  0.0 77.5 jit_solution(6423589051055024144)
XLA Ops:
  0.0 1.0 %copy-done = bf16[1,8,5,32,128]{4,3,2,1,0:T(8,128)(2,1)S(1)} copy-done((bf16[1,8,5,32,128]{4,3,2,1,0:T(8,128)(2,1)S(1)}, bf16[1,8,5,32,128]{4,3,2,1,0:T(8,128)(2,1)}, u32[]{:S(2)}) %copy-start) | copy-done | bytes 327704
  1.0 0.5 collective-permute-start
  1.5 0.1 collective-permute-start.7
  1.6 0.9 %collective-permute-done = bf16[4,5,32,128]{3,2,1,0:T(8,128)(2,1)S(1)} collective-permute-done((bf16[4,5,32,128]{3,2,1,0:T(8,128)(2,1)S(1)}, bf16[4,5,32,128]{3,2,1,0:T(8,128)(2,1)S(1)}, u32[]{:S(2)}, u32[]{:S(2)}) %collective-permute-start) | collective-permute-done | bytes 163872 | tf_op jit(solution)/shard_map/give/ppermute | solution.py:144
  2.5 0.7 fusion.3
  3.2 4.0 %collective-permute-start.9 = (bf16[2,1,5,32,128]{4,3,2,0,1:T(8,128)(2,1)S(1)}, bf16[2,1,5,32,128]{4,3,2,0,1:T(8,128)(2,1)S(1)}, u32[]{:S(2)}, u32[]{:S(2)}) collective-permute-start(bf16[2,1,5,32,128]{4,3,2,0,1:T(8,128)(2,1)S(1)} %get-tuple-element.25), channel_id=1, source_target_pairs={{0,2},{1,3},{2,0},{3,1},{4,6},{5,7},{6,4},{7,5},{8,10},{9,11},{10,... | collective-permute-start | bytes 245768 | tf_op jit(solution)/shard_map/z_0/ppermute | solution.py:144
  7.1 1.3 %collective-permute-start.10 = (bf16[2,1,5,32,128]{4,3,2,0,1:T(8,128)(2,1)S(1)}, bf16[2,1,5,32,128]{4,3,2,0,1:T(8,128)(2,1)S(1)}, u32[]{:S(2)}, u32[]{:S(2)}) collective-permute-start(bf16[2,1,5,32,128]{4,3,2,0,1:T(8,128)(2,1)S(1)} %get-tuple-element.25), channel_id=1, source_target_pairs={{0,3},{1,2},{2,1},{3,0},{4,7},{5,6},{6,5},{7,4},{8,11},{9,10},{10,... | collective-permute-start | bytes 245768 | tf_op jit(solution)/shard_map/z_0/ppermute | solution.py:144
  8.5 0.2 collective-permute-start.8
  8.7 1.8 %collective-permute-start.14 = (bf16[2,1,5,32,128]{4,3,2,0,1:T(8,128)(2,1)S(1)}, bf16[2,1,5,32,128]{4,3,2,0,1:T(8,128)(2,1)S(1)}, u32[]{:S(2)}, u32[]{:S(2)}) collective-permute-start(bf16[2,1,5,32,128]{4,3,2,0,1:T(8,128)(2,1)S(1)} %get-tuple-element.26), channel_id=1, source_target_pairs={{0,1},{1,0},{2,3},{3,2},{4,5},{5,4},{6,7},{7,6},{8,9},{9,8},{10,11... | collective-permute-start | bytes 245768 | tf_op jit(solution)/shard_map/z_1/ppermute | solution.py:144
  10.5 0.8 pad_maximum_fusion
  11.3 2.2 %collective-permute-done.9 = bf16[2,1,5,32,128]{4,3,2,0,1:T(8,128)(2,1)S(1)} collective-permute-done((bf16[2,1,5,32,128]{4,3,2,0,1:T(8,128)(2,1)S(1)}, bf16[2,1,5,32,128]{4,3,2,0,1:T(8,128)(2,1)S(1)}, u32[]{:S(2)}, u32[]{:S(2)}) %collective-permute-start.9) | collective-permute-done | bytes 81952 | tf_op jit(solution)/shard_map/z_0/ppermute | solution.py:144
  13.5 0.0 collective-permute-start.15
  13.5 0.8 %collective-permute-done.10 = bf16[2,1,5,32,128]{4,3,2,0,1:T(8,128)(2,1)S(1)} collective-permute-done((bf16[2,1,5,32,128]{4,3,2,0,1:T(8,128)(2,1)S(1)}, bf16[2,1,5,32,128]{4,3,2,0,1:T(8,128)(2,1)S(1)}, u32[]{:S(2)}, u32[]{:S(2)}) %collective-permute-start.10) | collective-permute-done | bytes 81952 | tf_op jit(solution)/shard_map/z_0/ppermute | solution.py:144
  14.3 2.8 %collective-permute-start.16 = (bf16[2,1,5,32,128]{4,3,2,0,1:T(8,128)(2,1)S(1)}, bf16[2,1,5,32,128]{4,3,2,0,1:T(8,128)(2,1)S(1)}, u32[]{:S(2)}, u32[]{:S(2)}) collective-permute-start(bf16[2,1,5,32,128]{4,3,2,0,1:T(8,128)(2,1)S(1)} %get-tuple-element.26), channel_id=1, source_target_pairs={{0,3},{1,2},{2,1},{3,0},{4,7},{5,6},{6,5},{7,4},{8,11},{9,10},{10,... | collective-permute-start | bytes 245768 | tf_op jit(solution)/shard_map/z_1/ppermute | solution.py:144
  17.1 0.0 collective-permute-done.8
  17.1 1.5 %collective-permute-start.1 = (bf16[2,4,5,32,128]{4,3,2,0,1:T(8,128)(2,1)}, bf16[2,4,5,32,128]{4,3,2,0,1:T(8,128)(2,1)}, u32[]{:S(2)}, u32[]{:S(2)}) collective-permute-start(bf16[2,4,5,32,128]{4,3,2,0,1:T(8,128)(2,1)} %pad_maximum_fusion), channel_id=1, source_target_pairs={{0,8},{1,9},{2,10},{3,11},{4,12},{5,13},{6,14},{7,15},{8,0},{9,1},... | collective-permute-start | bytes 983048 | tf_op jit(solution)/shard_map/x_own/ppermute | solution.py:144
  18.6 0.7 pad_maximum_fusion.2
  19.3 0.0 collective-permute-done.14
  19.3 2.0 %collective-permute-start.3 = (bf16[2,1,5,32,128]{4,3,2,0,1:T(8,128)(2,1)}, bf16[2,1,5,32,128]{4,3,2,0,1:T(8,128)(2,1)}, u32[]{:S(2)}, u32[]{:S(2)}) collective-permute-start(bf16[2,1,5,32,128]{4,3,2,0,1:T(8,128)(2,1)} %get-tuple-element.24), channel_id=1, source_target_pairs={{0,1},{1,0},{2,3},{3,2},{4,5},{5,4},{6,7},{7,6},{8,9},{9,8},{10,11... | collective-permute-start | bytes 245768 | tf_op jit(solution)/shard_map/z_3/ppermute | solution.py:144
  21.3 1.7 %collective-permute-done.15 = bf16[2,1,5,32,128]{4,3,2,0,1:T(8,128)(2,1)S(1)} collective-permute-done((bf16[2,1,5,32,128]{4,3,2,0,1:T(8,128)(2,1)S(1)}, bf16[2,1,5,32,128]{4,3,2,0,1:T(8,128)(2,1)S(1)}, u32[]{:S(2)}, u32[]{:S(2)}) %collective-permute-start.15) | collective-permute-done | bytes 81952 | tf_op jit(solution)/shard_map/z_1/ppermute | solution.py:144
  23.0 1.5 %collective-permute-start.11 = (bf16[3,2,1,5,32,128]{5,4,3,1,2,0:T(8,128)(2,1)}, bf16[3,2,1,5,32,128]{5,4,3,1,2,0:T(8,128)(2,1)}, u32[]{:S(2)}, u32[]{:S(2)}) collective-permute-start(bf16[3,2,1,5,32,128]{5,4,3,1,2,0:T(8,128)(2,1)} %get-tuple-element.31), channel_id=1, source_target_pairs={{0,8},{1,9},{2,10},{3,11},{4,12},{5,13},{6,14},{7,15},{8,0},{9,1},... | collective-permute-start | bytes 737288 | tf_op jit(solution)/shard_map/x_0/ppermute | solution.py:144
  24.5 0.0 collective-permute-done.16
  24.5 0.7 pad_maximum_fusion.3
  25.3 0.5 collective-permute-start.17
  25.8 0.1 copy.11
  25.9 0.0 collective-permute-done.3
  25.9 1.3 %collective-permute-start.4 = (bf16[2,1,5,32,128]{4,3,2,0,1:T(8,128)(2,1)}, bf16[2,1,5,32,128]{4,3,2,0,1:T(8,128)(2,1)S(1)}, u32[]{:S(2)}, u32[]{:S(2)}) collective-permute-start(bf16[2,1,5,32,128]{4,3,2,0,1:T(8,128)(2,1)} %get-tuple-element.24), channel_id=1, source_target_pairs={{0,2},{1,3},{2,0},{3,1},{4,6},{5,7},{6,4},{7,5},{8,10},{9,11},{10,... | collective-permute-start | bytes 245768 | tf_op jit(solution)/shard_map/z_3/ppermute | solution.py:144
  27.2 0.8 collective-permute-done.1
  28.0 1.8 %collective-permute-start.5 = (bf16[2,1,5,32,128]{4,3,2,0,1:T(8,128)(2,1)}, bf16[2,1,5,32,128]{4,3,2,0,1:T(8,128)(2,1)S(1)}, u32[]{:S(2)}, u32[]{:S(2)}) collective-permute-start(bf16[2,1,5,32,128]{4,3,2,0,1:T(8,128)(2,1)} %get-tuple-element.24), channel_id=1, source_target_pairs={{0,3},{1,2},{2,1},{3,0},{4,7},{5,6},{6,5},{7,4},{8,11},{9,10},{10,... | collective-permute-start | bytes 245768 | tf_op jit(solution)/shard_map/z_3/ppermute | solution.py:144
  29.8 0.1 pad_add_fusion.refs_1_
  29.9 3.7 %collective-permute-done.4 = bf16[2,1,5,32,128]{4,3,2,0,1:T(8,128)(2,1)S(1)} collective-permute-done((bf16[2,1,5,32,128]{4,3,2,0,1:T(8,128)(2,1)}, bf16[2,1,5,32,128]{4,3,2,0,1:T(8,128)(2,1)S(1)}, u32[]{:S(2)}, u32[]{:S(2)}) %collective-permute-start.4) | collective-permute-done | bytes 81952 | tf_op jit(solution)/shard_map/z_3/ppermute | solution.py:144
  33.6 0.0 collective-permute-start.20
  33.6 1.1 %collective-permute-done.5 = bf16[2,1,5,32,128]{4,3,2,0,1:T(8,128)(2,1)S(1)} collective-permute-done((bf16[2,1,5,32,128]{4,3,2,0,1:T(8,128)(2,1)}, bf16[2,1,5,32,128]{4,3,2,0,1:T(8,128)(2,1)S(1)}, u32[]{:S(2)}, u32[]{:S(2)}) %collective-permute-start.5) | collective-permute-done | bytes 81952 | tf_op jit(solution)/shard_map/z_3/ppermute | solution.py:144
  34.7 3.4 %collective-permute-start.2 = (bf16[2,4,5,32,128]{4,3,2,0,1:T(8,128)(2,1)}, bf16[2,4,5,32,128]{4,3,2,0,1:T(8,128)(2,1)S(1)}, u32[]{:S(2)}, u32[]{:S(2)}) collective-permute-start(bf16[2,4,5,32,128]{4,3,2,0,1:T(8,128)(2,1)} %collective-permute-done.1), channel_id=1, source_target_pairs={{0,16},{1,17},{2,18},{3,19},{4,20},{5,21},{6,22},{7,23},{24,8},{25... | collective-permute-start | bytes 983048 | tf_op jit(solution)/shard_map/y_own/ppermute | solution.py:144
  38.1 0.0 collective-permute-done.11
  38.1 1.3 %collective-permute-start.12 = (bf16[3,2,1,5,32,128]{5,4,3,1,2,0:T(8,128)(2,1)}, bf16[3,2,1,5,32,128]{5,4,3,1,2,0:T(8,128)(2,1)S(1)}, u32[]{:S(2)}, u32[]{:S(2)}) collective-permute-start(bf16[3,2,1,5,32,128]{5,4,3,1,2,0:T(8,128)(2,1)} %collective-permute-done.11), channel_id=1, source_target_pairs={{0,16},{1,17},{2,18},{3,19},{4,20},{5,21},{6,22},{7,23},{24,8},{25... | collective-permute-start | bytes 737288 | tf_op jit(solution)/shard_map/y_0/ppermute | solution.py:144
  39.5 1.0 %copy.33.refs_5_.refs_3_ = bf16[2,4,5,32,128]{4,3,2,1,0:T(8,128)(2,1)S(1)} copy(bf16[2,4,5,32,128]{4,3,2,0,1:T(8,128)(2,1)} %pad_maximum_fusion) | data formatting | bytes 655360 | tf_op jit(solution)/shard_map/stack | solution.py:164
  40.5 0.0 collective-permute-done.17
  40.5 1.5 %collective-permute-start.21 = (bf16[2,1,5,32,128]{4,3,2,0,1:T(8,128)(2,1)S(1)}, bf16[2,1,5,32,128]{4,3,2,0,1:T(8,128)(2,1)S(1)}, u32[]{:S(2)}, u32[]{:S(2)}) collective-permute-start(bf16[2,1,5,32,128]{4,3,2,0,1:T(8,128)(2,1)S(1)} %get-tuple-element.20), channel_id=1, source_target_pairs={{0,2},{1,3},{2,0},{3,1},{4,6},{5,7},{6,4},{7,5},{8,10},{9,11},{10,... | collective-permute-start | bytes 245768 | tf_op jit(solution)/shard_map/z_2/ppermute | solution.py:144
  42.0 0.0 collective-permute-done.20
  42.0 2.1 %collective-permute-start.22 = (bf16[2,1,5,32,128]{4,3,2,0,1:T(8,128)(2,1)S(1)}, bf16[2,1,5,32,128]{4,3,2,0,1:T(8,128)(2,1)S(1)}, u32[]{:S(2)}, u32[]{:S(2)}) collective-permute-start(bf16[2,1,5,32,128]{4,3,2,0,1:T(8,128)(2,1)S(1)} %get-tuple-element.20), channel_id=1, source_target_pairs={{0,3},{1,2},{2,1},{3,0},{4,7},{5,6},{6,5},{7,4},{8,11},{9,10},{10,... | collective-permute-start | bytes 245768 | tf_op jit(solution)/shard_map/z_2/ppermute | solution.py:144
  44.1 0.9 %pad_maximum_fusion.1.refs_6_ = bf16[3,2,1,5,32,128]{5,4,3,2,1,0:T(8,128)(2,1)S(1)} fusion(bf16[1,2,1,5,32,128]{5,4,3,2,1,0:T(8,128)(2,1)S(1)} %bitcast.45, bf16[1,2,1,5,32,128]{5,4,3,2,1,0:T(8,128)(2,1)S(1)} %bitcast.43, bf16[1,2,1,5,32,128]{5,4,3,2,1,0:T(8,128)(2,1)} %bitcast.5), kind=kLoop, calls=%fused_computation.9 | loop fusion | flops 245760 | bytes 491520 | tf_op jit(solution)/shard_map/stack | solution.py:185
  45.0 1.0 %copy.34.refs_6_.refs_4_ = bf16[2,4,5,32,128]{4,3,2,1,0:T(8,128)(2,1)S(1)} copy(bf16[2,4,5,32,128]{4,3,2,0,1:T(8,128)(2,1)} %collective-permute-done.1) | data formatting | bytes 655360 | tf_op jit(solution)/shard_map/x_own/ppermute | solution.py:144
  46.0 0.7 collective-permute-done.21
  46.8 0.0 collective-permute-start.6
  46.8 1.6 %collective-permute-done.22 = bf16[2,1,5,32,128]{4,3,2,0,1:T(8,128)(2,1)S(1)} collective-permute-done((bf16[2,1,5,32,128]{4,3,2,0,1:T(8,128)(2,1)S(1)}, bf16[2,1,5,32,128]{4,3,2,0,1:T(8,128)(2,1)S(1)}, u32[]{:S(2)}, u32[]{:S(2)}) %collective-permute-start.22) | collective-permute-done | bytes 81952 | tf_op jit(solution)/shard_map/z_2/ppermute | solution.py:144
  48.3 1.3 %collective-permute-start.18 = (bf16[3,2,1,5,32,128]{5,4,3,1,2,0:T(8,128)(2,1)S(1)}, bf16[3,2,1,5,32,128]{5,4,3,1,2,0:T(8,128)(2,1)S(1)}, u32[]{:S(2)}, u32[]{:S(2)}) collective-permute-start(bf16[3,2,1,5,32,128]{5,4,3,1,2,0:T(8,128)(2,1)S(1)} %collective-permute-done.17), channel_id=1, source_target_pairs={{0,16},{1,17},{2,18},{3,19},{4,20},{5,21},{6,22},{7,23},{24,8},{25... | collective-permute-start | bytes 737288 | tf_op jit(solution)/shard_map/y_1/ppermute | solution.py:144
  49.7 0.0 collective-permute-done.2
  49.7 0.1 collective-permute-start.23
  49.8 0.0 collective-permute-done.6.refs_2_.refs_1_
  49.8 0.0 collective-permute-done.7.refs_4_.refs_2_
  49.9 4.2 %shard_map.46 = (f32[4,384,384]{2,1,0:T(8,128)S(1)}, f32[4,384,384]{2,1,0:T(8,128)S(1)}) custom-call(s32[8]{0:T(128)S(1)} %compare_select_fusion.3.refs_0_, s32[4,4]{1,0:T(4,128)S(1)} %pad_add_fusion.refs_1_, s32[4,4]{1,0:T(4,128)S(1)} %collective-permute-done.6.refs_2_.refs_1_, bf16[4,384,384]{2,1,0:T(8,128)(2,1)S(1)} %copy-done.1, ...), custom_call_target="tpu_custom_call" | custom-call | flops 1811939328 | bytes 8388608 | tf_op jit(solution)/shard_map/pallas_call | solution.py:104
  54.1 2.6 %collective-permute-start.13 = (bf16[3,2,1,5,32,128]{5,4,3,2,1,0:T(8,128)(2,1)S(1)}, bf16[3,2,1,5,32,128]{5,4,3,2,1,0:T(8,128)(2,1)S(1)}, u32[]{:S(2)}, u32[]{:S(2)}) collective-permute-start(bf16[3,2,1,5,32,128]{5,4,3,2,1,0:T(8,128)(2,1)S(1)} %pad_maximum_fusion.1.refs_6_), channel_id=1, source_target_pairs={{0,8},{1,9},{2,10},{3,11},{4,12},{5,13},{6,14},{7,15},{8,0},{9,1},... | collective-permute-start | bytes 737288 | tf_op jit(solution)/shard_map/x_3/ppermute | solution.py:144
  56.7 0.1 collective-permute-done.23
  56.8 1.8 %collective-permute-start.24 = (bf16[3,2,1,5,32,128]{5,4,3,1,2,0:T(8,128)(2,1)S(1)}, bf16[3,2,1,5,32,128]{5,4,3,1,2,0:T(8,128)(2,1)S(1)}, u32[]{:S(2)}, u32[]{:S(2)}) collective-permute-start(bf16[3,2,1,5,32,128]{5,4,3,1,2,0:T(8,128)(2,1)S(1)} %collective-permute-done.23), channel_id=1, source_target_pairs={{0,16},{1,17},{2,18},{3,19},{4,20},{5,21},{6,22},{7,23},{24,8},{25... | collective-permute-start | bytes 737288 | tf_op jit(solution)/shard_map/y_2/ppermute | solution.py:144
  58.6 0.0 collective-permute-done.18
  58.6 3.9 %shard_map.47 = (f32[4,384,384]{2,1,0:T(8,128)S(1)}, f32[4,384,384]{2,1,0:T(8,128)S(1)}) custom-call(s32[8]{0:T(128)S(1)} %compare_select_fusion.3.refs_0_, s32[4,4]{1,0:T(4,128)S(1)} %pad_add_fusion.refs_1_, s32[4,4]{1,0:T(4,128)S(1)} %collective-permute-done.6.refs_2_.refs_1_, ...), custom_call_target="tpu_custom_call", output_to_operand_aliasing={{0}: (11, {}), {1}: (12, {})} | custom-call | flops 1811939328 | bytes 8388608 | tf_op jit(solution)/shard_map/pallas_call | solution.py:104
  62.5 2.3 %collective-permute-start.19 = (bf16[3,2,1,5,32,128]{5,4,3,2,1,0:T(8,128)(2,1)S(1)}, bf16[3,2,1,5,32,128]{5,4,3,2,1,0:T(8,128)(2,1)S(1)}, u32[]{:S(2)}, u32[]{:S(2)}) collective-permute-start(bf16[3,2,1,5,32,128]{5,4,3,2,1,0:T(8,128)(2,1)S(1)} %collective-permute-done.13.refs_7_), channel_id=1, source_target_pairs={{0,16},{1,17},{2,18},{3,19},{4,20},{5,21},{6,22},{7,23},{24,8},{25... | collective-permute-start | bytes 737288 | tf_op jit(solution)/shard_map/y_3/ppermute | solution.py:144
  64.9 3.9 %shard_map.48 = (f32[4,384,384]{2,1,0:T(8,128)S(1)}, f32[4,384,384]{2,1,0:T(8,128)S(1)}) custom-call(s32[8]{0:T(128)S(1)} %compare_select_fusion.3.refs_0_, s32[4,4]{1,0:T(4,128)S(1)} %pad_add_fusion.refs_1_, s32[4,4]{1,0:T(4,128)S(1)} %collective-permute-done.6.refs_2_.refs_1_, ...), custom_call_target="tpu_custom_call", output_to_operand_aliasing={{0}: (11, {}), {1}: (12, {})} | custom-call | flops 1811939328 | bytes 8388608 | tf_op jit(solution)/shard_map/pallas_call | solution.py:104
  68.8 2.4 %shard_map.50 = f32[4,384,384]{2,1,0:T(8,128)S(1)} custom-call(s32[8]{0:T(128)S(1)} %compare_select_fusion.3.refs_0_, s32[4,4]{1,0:T(4,128)S(1)} %collective-permute-done.6.refs_2_.refs_1_, bf16[4,384,384]{2,1,0:T(8,128)(2,1)S(1)} %collective-permute-done.7.refs_4_.refs_2_, ...), custom_call_target="tpu_custom_call", output_to_operand_aliasing={{}: (9, {})} | custom-call | flops 905969664 | bytes 8388608 | tf_op jit(solution)/shard_map/pallas_call | solution.py:104
  71.2 0.1 collective-permute-start.25
  71.3 2.1 %shard_map.49 = f32[4,384,384]{2,1,0:T(8,128)S(1)} custom-call(s32[8]{0:T(128)S(1)} %compare_select_fusion.3.refs_0_, s32[4,4]{1,0:T(4,128)S(1)} %pad_add_fusion.refs_1_, bf16[4,384,384]{2,1,0:T(8,128)(2,1)S(1)} %copy-done.1, bf16[2,4,5,32,128]{4,3,2,1,0:T(8,128)(2,1)S(1)} %copy.33.refs_5_.refs_3_, ...), custom_call_target="tpu_custom_call", output_to_operand_aliasing={{}: (9, {})} | custom-call | flops 905969664 | bytes 8388608 | tf_op jit(solution)/shard_map/pallas_call | solution.py:104
  73.4 2.5 %collective-permute-done.25 = f32[4,384,384]{2,1,0:T(8,128)S(1)} collective-permute-done((f32[4,384,384]{2,1,0:T(8,128)S(1)}, f32[4,384,384]{2,1,0:T(8,128)S(1)}, u32[]{:S(2)}, u32[]{:S(2)}) %collective-permute-start.25) | collective-permute-done | bytes 2359328 | tf_op jit(solution)/shard_map/sums/ppermute | solution.py:144
  75.8 1.6 %add.16 = f32[4,384,384]{2,1,0:T(8,128)} add(f32[4,384,384]{2,1,0:T(8,128)S(1)} %shard_map.49, f32[4,384,384]{2,1,0:T(8,128)S(1)} %collective-permute-done.25) | non-fusion elementwise | flops 589824 | bytes 7077888 | tf_op jit(solution)/shard_map/add | solution.py:227
  (17 shorter events, 0.1 us)
Async XLA Ops:
  0.0 1.0 %copy-start = (bf16[1,8,5,32,128]{4,3,2,1,0:T(8,128)(2,1)S(1)}, bf16[1,8,5,32,128]{4,3,2,1,0:T(8,128)(2,1)}, u32[]{:S(2)}) copy-start(bf16[1,8,5,32,128]{4,3,2,1,0:T(8,128)(2,1)} %param.7) | copy-start | bytes 983044
  0.0 25.8 %copy-start.3 = (s32[4]{0:T(128)S(1)}, s32[4]{0:T(128)}, u32[]{:S(2)}) copy-start(s32[4]{0:T(128)} %param.6) | copy-start | bytes 52
  0.0 29.8 %copy-start.2 = (s32[4,3]{1,0:T(4,128)S(1)}, s32[4,3]{1,0:T(4,128)}, u32[]{:S(2)}) copy-start(s32[4,3]{1,0:T(4,128)} %param.5) | copy-start | bytes 148
  1.0 1.5 %collective-permute-start = (bf16[4,5,32,128]{3,2,1,0:T(8,128)(2,1)S(1)}, bf16[4,5,32,128]{3,2,1,0:T(8,128)(2,1)S(1)}, u32[]{:S(2)}, u32[]{:S(2)}) collective-permute-start(bf16[4,5,32,128]{3,2,1,0:T(8,128)(2,1)S(1)} %dynamic-slice_bitcast_fusion), channel_id=1, source_target_pairs={{0,4},{1,5},{2,6},{3,7},{4,0},{5,1},{6,2},{7,3},{8,12},{9,13},{10,... | collective-permute-start | bytes 491528 | tf_op jit(solution)/shard_map/give/ppermute | solution.py:144
  1.5 48.3 %collective-permute-start.7 = (bf16[4,384,384]{2,1,0:T(8,128)(2,1)}, bf16[4,384,384]{2,1,0:T(8,128)(2,1)S(1)}, u32[]{:S(2)}, u32[]{:S(2)}) collective-permute-start(bf16[4,384,384]{2,1,0:T(8,128)(2,1)} %refs_2_.1), channel_id=1, source_target_pairs={{0,4},{1,5},{2,6},{3,7},{4,0},{5,1},{6,2},{7,3},{8,12},{9,13},{10,... | collective-permute-start | bytes 3538952 | tf_op jit(solution)/shard_map/p_far/ppermute | solution.py:144
  3.2 10.3 %collective-permute-start.9 = (bf16[2,1,5,32,128]{4,3,2,0,1:T(8,128)(2,1)S(1)}, bf16[2,1,5,32,128]{4,3,2,0,1:T(8,128)(2,1)S(1)}, u32[]{:S(2)}, u32[]{:S(2)}) collective-permute-start(bf16[2,1,5,32,128]{4,3,2,0,1:T(8,128)(2,1)S(1)} %get-tuple-element.25), channel_id=1, source_target_pairs={{0,2},{1,3},{2,0},{3,1},{4,6},{5,7},{6,4},{7,5},{8,10},{9,11},{10,... | collective-permute-start | bytes 245768 | tf_op jit(solution)/shard_map/z_0/ppermute | solution.py:144
  7.1 7.1 %collective-permute-start.10 = (bf16[2,1,5,32,128]{4,3,2,0,1:T(8,128)(2,1)S(1)}, bf16[2,1,5,32,128]{4,3,2,0,1:T(8,128)(2,1)S(1)}, u32[]{:S(2)}, u32[]{:S(2)}) collective-permute-start(bf16[2,1,5,32,128]{4,3,2,0,1:T(8,128)(2,1)S(1)} %get-tuple-element.25), channel_id=1, source_target_pairs={{0,3},{1,2},{2,1},{3,0},{4,7},{5,6},{6,5},{7,4},{8,11},{9,10},{10,... | collective-permute-start | bytes 245768 | tf_op jit(solution)/shard_map/z_0/ppermute | solution.py:144
  8.5 8.6 %collective-permute-start.8 = (bf16[2,1,5,32,128]{4,3,2,0,1:T(8,128)(2,1)S(1)}, bf16[2,1,5,32,128]{4,3,2,0,1:T(8,128)(2,1)S(1)}, u32[]{:S(2)}, u32[]{:S(2)}) collective-permute-start(bf16[2,1,5,32,128]{4,3,2,0,1:T(8,128)(2,1)S(1)} %get-tuple-element.25), channel_id=1, source_target_pairs={{0,1},{1,0},{2,3},{3,2},{4,5},{5,4},{6,7},{7,6},{8,9},{9,8},{10,11... | collective-permute-start | bytes 245768 | tf_op jit(solution)/shard_map/z_0/ppermute | solution.py:144
  8.7 10.6 %collective-permute-start.14 = (bf16[2,1,5,32,128]{4,3,2,0,1:T(8,128)(2,1)S(1)}, bf16[2,1,5,32,128]{4,3,2,0,1:T(8,128)(2,1)S(1)}, u32[]{:S(2)}, u32[]{:S(2)}) collective-permute-start(bf16[2,1,5,32,128]{4,3,2,0,1:T(8,128)(2,1)S(1)} %get-tuple-element.26), channel_id=1, source_target_pairs={{0,1},{1,0},{2,3},{3,2},{4,5},{5,4},{6,7},{7,6},{8,9},{9,8},{10,11... | collective-permute-start | bytes 245768 | tf_op jit(solution)/shard_map/z_1/ppermute | solution.py:144
  13.5 9.6 %collective-permute-start.15 = (bf16[2,1,5,32,128]{4,3,2,0,1:T(8,128)(2,1)S(1)}, bf16[2,1,5,32,128]{4,3,2,0,1:T(8,128)(2,1)S(1)}, u32[]{:S(2)}, u32[]{:S(2)}) collective-permute-start(bf16[2,1,5,32,128]{4,3,2,0,1:T(8,128)(2,1)S(1)} %get-tuple-element.26), channel_id=1, source_target_pairs={{0,2},{1,3},{2,0},{3,1},{4,6},{5,7},{6,4},{7,5},{8,10},{9,11},{10,... | collective-permute-start | bytes 245768 | tf_op jit(solution)/shard_map/z_1/ppermute | solution.py:144
  14.3 10.3 %collective-permute-start.16 = (bf16[2,1,5,32,128]{4,3,2,0,1:T(8,128)(2,1)S(1)}, bf16[2,1,5,32,128]{4,3,2,0,1:T(8,128)(2,1)S(1)}, u32[]{:S(2)}, u32[]{:S(2)}) collective-permute-start(bf16[2,1,5,32,128]{4,3,2,0,1:T(8,128)(2,1)S(1)} %get-tuple-element.26), channel_id=1, source_target_pairs={{0,3},{1,2},{2,1},{3,0},{4,7},{5,6},{6,5},{7,4},{8,11},{9,10},{10,... | collective-permute-start | bytes 245768 | tf_op jit(solution)/shard_map/z_1/ppermute | solution.py:144
  17.1 10.9 %collective-permute-start.1 = (bf16[2,4,5,32,128]{4,3,2,0,1:T(8,128)(2,1)}, bf16[2,4,5,32,128]{4,3,2,0,1:T(8,128)(2,1)}, u32[]{:S(2)}, u32[]{:S(2)}) collective-permute-start(bf16[2,4,5,32,128]{4,3,2,0,1:T(8,128)(2,1)} %pad_maximum_fusion), channel_id=1, source_target_pairs={{0,8},{1,9},{2,10},{3,11},{4,12},{5,13},{6,14},{7,15},{8,0},{9,1},... | collective-permute-start | bytes 983048 | tf_op jit(solution)/shard_map/x_own/ppermute | solution.py:144
  18.6 31.3 %copy-start.1 = (bf16[4,384,384]{2,1,0:T(8,128)(2,1)S(1)}, bf16[4,384,384]{2,1,0:T(8,128)(2,1)}, u32[]{:S(2)}) copy-start(bf16[4,384,384]{2,1,0:T(8,128)(2,1)} %refs_2_.1) | copy-start | bytes 3538948
  19.3 6.6 %collective-permute-start.3 = (bf16[2,1,5,32,128]{4,3,2,0,1:T(8,128)(2,1)}, bf16[2,1,5,32,128]{4,3,2,0,1:T(8,128)(2,1)}, u32[]{:S(2)}, u32[]{:S(2)}) collective-permute-start(bf16[2,1,5,32,128]{4,3,2,0,1:T(8,128)(2,1)} %get-tuple-element.24), channel_id=1, source_target_pairs={{0,1},{1,0},{2,3},{3,2},{4,5},{5,4},{6,7},{7,6},{8,9},{9,8},{10,11... | collective-permute-start | bytes 245768 | tf_op jit(solution)/shard_map/z_3/ppermute | solution.py:144
  23.0 15.1 %collective-permute-start.11 = (bf16[3,2,1,5,32,128]{5,4,3,1,2,0:T(8,128)(2,1)}, bf16[3,2,1,5,32,128]{5,4,3,1,2,0:T(8,128)(2,1)}, u32[]{:S(2)}, u32[]{:S(2)}) collective-permute-start(bf16[3,2,1,5,32,128]{5,4,3,1,2,0:T(8,128)(2,1)} %get-tuple-element.31), channel_id=1, source_target_pairs={{0,8},{1,9},{2,10},{3,11},{4,12},{5,13},{6,14},{7,15},{8,0},{9,1},... | collective-permute-start | bytes 737288 | tf_op jit(solution)/shard_map/x_0/ppermute | solution.py:144
  25.3 15.2 %collective-permute-start.17 = (bf16[3,2,1,5,32,128]{5,4,3,1,2,0:T(8,128)(2,1)}, bf16[3,2,1,5,32,128]{5,4,3,1,2,0:T(8,128)(2,1)S(1)}, u32[]{:S(2)}, u32[]{:S(2)}) collective-permute-start(bf16[3,2,1,5,32,128]{5,4,3,1,2,0:T(8,128)(2,1)} %get-tuple-element.29), channel_id=1, source_target_pairs={{0,8},{1,9},{2,10},{3,11},{4,12},{5,13},{6,14},{7,15},{8,0},{9,1},... | collective-permute-start | bytes 737288 | tf_op jit(solution)/shard_map/x_1/ppermute | solution.py:144
  25.9 7.7 %collective-permute-start.4 = (bf16[2,1,5,32,128]{4,3,2,0,1:T(8,128)(2,1)}, bf16[2,1,5,32,128]{4,3,2,0,1:T(8,128)(2,1)S(1)}, u32[]{:S(2)}, u32[]{:S(2)}) collective-permute-start(bf16[2,1,5,32,128]{4,3,2,0,1:T(8,128)(2,1)} %get-tuple-element.24), channel_id=1, source_target_pairs={{0,2},{1,3},{2,0},{3,1},{4,6},{5,7},{6,4},{7,5},{8,10},{9,11},{10,... | collective-permute-start | bytes 245768 | tf_op jit(solution)/shard_map/z_3/ppermute | solution.py:144
  28.0 6.7 %collective-permute-start.5 = (bf16[2,1,5,32,128]{4,3,2,0,1:T(8,128)(2,1)}, bf16[2,1,5,32,128]{4,3,2,0,1:T(8,128)(2,1)S(1)}, u32[]{:S(2)}, u32[]{:S(2)}) collective-permute-start(bf16[2,1,5,32,128]{4,3,2,0,1:T(8,128)(2,1)} %get-tuple-element.24), channel_id=1, source_target_pairs={{0,3},{1,2},{2,1},{3,0},{4,7},{5,6},{6,5},{7,4},{8,11},{9,10},{10,... | collective-permute-start | bytes 245768 | tf_op jit(solution)/shard_map/z_3/ppermute | solution.py:144
  33.6 8.4 %collective-permute-start.20 = (bf16[2,1,5,32,128]{4,3,2,0,1:T(8,128)(2,1)S(1)}, bf16[2,1,5,32,128]{4,3,2,0,1:T(8,128)(2,1)S(1)}, u32[]{:S(2)}, u32[]{:S(2)}) collective-permute-start(bf16[2,1,5,32,128]{4,3,2,0,1:T(8,128)(2,1)S(1)} %get-tuple-element.20), channel_id=1, source_target_pairs={{0,1},{1,0},{2,3},{3,2},{4,5},{5,4},{6,7},{7,6},{8,9},{9,8},{10,11... | collective-permute-start | bytes 245768 | tf_op jit(solution)/shard_map/z_2/ppermute | solution.py:144
  34.7 15.0 %collective-permute-start.2 = (bf16[2,4,5,32,128]{4,3,2,0,1:T(8,128)(2,1)}, bf16[2,4,5,32,128]{4,3,2,0,1:T(8,128)(2,1)S(1)}, u32[]{:S(2)}, u32[]{:S(2)}) collective-permute-start(bf16[2,4,5,32,128]{4,3,2,0,1:T(8,128)(2,1)} %collective-permute-done.1), channel_id=1, source_target_pairs={{0,16},{1,17},{2,18},{3,19},{4,20},{5,21},{6,22},{7,23},{24,8},{25... | collective-permute-start | bytes 983048 | tf_op jit(solution)/shard_map/y_own/ppermute | solution.py:144
  38.1 11.7 %collective-permute-start.12 = (bf16[3,2,1,5,32,128]{5,4,3,1,2,0:T(8,128)(2,1)}, bf16[3,2,1,5,32,128]{5,4,3,1,2,0:T(8,128)(2,1)S(1)}, u32[]{:S(2)}, u32[]{:S(2)}) collective-permute-start(bf16[3,2,1,5,32,128]{5,4,3,1,2,0:T(8,128)(2,1)} %collective-permute-done.11), channel_id=1, source_target_pairs={{0,16},{1,17},{2,18},{3,19},{4,20},{5,21},{6,22},{7,23},{24,8},{25... | collective-permute-start | bytes 737288 | tf_op jit(solution)/shard_map/y_0/ppermute | solution.py:144
  40.5 6.3 %collective-permute-start.21 = (bf16[2,1,5,32,128]{4,3,2,0,1:T(8,128)(2,1)S(1)}, bf16[2,1,5,32,128]{4,3,2,0,1:T(8,128)(2,1)S(1)}, u32[]{:S(2)}, u32[]{:S(2)}) collective-permute-start(bf16[2,1,5,32,128]{4,3,2,0,1:T(8,128)(2,1)S(1)} %get-tuple-element.20), channel_id=1, source_target_pairs={{0,2},{1,3},{2,0},{3,1},{4,6},{5,7},{6,4},{7,5},{8,10},{9,11},{10,... | collective-permute-start | bytes 245768 | tf_op jit(solution)/shard_map/z_2/ppermute | solution.py:144
  42.0 6.3 %collective-permute-start.22 = (bf16[2,1,5,32,128]{4,3,2,0,1:T(8,128)(2,1)S(1)}, bf16[2,1,5,32,128]{4,3,2,0,1:T(8,128)(2,1)S(1)}, u32[]{:S(2)}, u32[]{:S(2)}) collective-permute-start(bf16[2,1,5,32,128]{4,3,2,0,1:T(8,128)(2,1)S(1)} %get-tuple-element.20), channel_id=1, source_target_pairs={{0,3},{1,2},{2,1},{3,0},{4,7},{5,6},{6,5},{7,4},{8,11},{9,10},{10,... | collective-permute-start | bytes 245768 | tf_op jit(solution)/shard_map/z_2/ppermute | solution.py:144
  46.8 3.1 %collective-permute-start.6 = (s32[4,4]{1,0:T(4,128)S(1)}, s32[4,4]{1,0:T(4,128)S(1)}, u32[]{:S(2)}, u32[]{:S(2)}) collective-permute-start(s32[4,4]{1,0:T(4,128)S(1)} %pad_add_fusion.refs_1_), channel_id=1, source_target_pairs={{0,4},{1,5},{2,6},{3,7},{4,0},{5,1},{6,2},{7,3},{8,12},{9,13},{10,... | collective-permute-start | bytes 200 | tf_op jit(solution)/shard_map/p_info/ppermute | solution.py:144
  48.3 10.3 %collective-permute-start.18 = (bf16[3,2,1,5,32,128]{5,4,3,1,2,0:T(8,128)(2,1)S(1)}, bf16[3,2,1,5,32,128]{5,4,3,1,2,0:T(8,128)(2,1)S(1)}, u32[]{:S(2)}, u32[]{:S(2)}) collective-permute-start(bf16[3,2,1,5,32,128]{5,4,3,1,2,0:T(8,128)(2,1)S(1)} %collective-permute-done.17), channel_id=1, source_target_pairs={{0,16},{1,17},{2,18},{3,19},{4,20},{5,21},{6,22},{7,23},{24,8},{25... | collective-permute-start | bytes 737288 | tf_op jit(solution)/shard_map/y_1/ppermute | solution.py:144
  49.7 7.1 %collective-permute-start.23 = (bf16[3,2,1,5,32,128]{5,4,3,1,2,0:T(8,128)(2,1)S(1)}, bf16[3,2,1,5,32,128]{5,4,3,1,2,0:T(8,128)(2,1)S(1)}, u32[]{:S(2)}, u32[]{:S(2)}) collective-permute-start(bf16[3,2,1,5,32,128]{5,4,3,1,2,0:T(8,128)(2,1)S(1)} %get-tuple-element.27), channel_id=1, source_target_pairs={{0,8},{1,9},{2,10},{3,11},{4,12},{5,13},{6,14},{7,15},{8,0},{9,1},... | collective-permute-start | bytes 737288 | tf_op jit(solution)/shard_map/x_2/ppermute | solution.py:144
  54.1 8.4 %collective-permute-start.13 = (bf16[3,2,1,5,32,128]{5,4,3,2,1,0:T(8,128)(2,1)S(1)}, bf16[3,2,1,5,32,128]{5,4,3,2,1,0:T(8,128)(2,1)S(1)}, u32[]{:S(2)}, u32[]{:S(2)}) collective-permute-start(bf16[3,2,1,5,32,128]{5,4,3,2,1,0:T(8,128)(2,1)S(1)} %pad_maximum_fusion.1.refs_6_), channel_id=1, source_target_pairs={{0,8},{1,9},{2,10},{3,11},{4,12},{5,13},{6,14},{7,15},{8,0},{9,1},... | collective-permute-start | bytes 737288 | tf_op jit(solution)/shard_map/x_3/ppermute | solution.py:144
  56.8 8.1 %collective-permute-start.24 = (bf16[3,2,1,5,32,128]{5,4,3,1,2,0:T(8,128)(2,1)S(1)}, bf16[3,2,1,5,32,128]{5,4,3,1,2,0:T(8,128)(2,1)S(1)}, u32[]{:S(2)}, u32[]{:S(2)}) collective-permute-start(bf16[3,2,1,5,32,128]{5,4,3,1,2,0:T(8,128)(2,1)S(1)} %collective-permute-done.23), channel_id=1, source_target_pairs={{0,16},{1,17},{2,18},{3,19},{4,20},{5,21},{6,22},{7,23},{24,8},{25... | collective-permute-start | bytes 737288 | tf_op jit(solution)/shard_map/y_2/ppermute | solution.py:144
  62.5 6.3 %collective-permute-start.19 = (bf16[3,2,1,5,32,128]{5,4,3,2,1,0:T(8,128)(2,1)S(1)}, bf16[3,2,1,5,32,128]{5,4,3,2,1,0:T(8,128)(2,1)S(1)}, u32[]{:S(2)}, u32[]{:S(2)}) collective-permute-start(bf16[3,2,1,5,32,128]{5,4,3,2,1,0:T(8,128)(2,1)S(1)} %collective-permute-done.13.refs_7_), channel_id=1, source_target_pairs={{0,16},{1,17},{2,18},{3,19},{4,20},{5,21},{6,22},{7,23},{24,8},{25... | collective-permute-start | bytes 737288 | tf_op jit(solution)/shard_map/y_3/ppermute | solution.py:144
  71.2 4.6 %collective-permute-start.25 = (f32[4,384,384]{2,1,0:T(8,128)S(1)}, f32[4,384,384]{2,1,0:T(8,128)S(1)}, u32[]{:S(2)}, u32[]{:S(2)}) collective-permute-start(f32[4,384,384]{2,1,0:T(8,128)S(1)} %shard_map.50), channel_id=1, source_target_pairs={{0,4},{1,5},{2,6},{3,7},{4,0},{5,1},{6,2},{7,3},{8,12},{9,13},{10,... | collective-permute-start | bytes 7077896 | tf_op jit(solution)/shard_map/sums/ppermute | solution.py:144
